TPU v7x, 128 devices: a whole 4x4x4 slice. The times are simulated.
128 devices in a mesh: gx: 8 (over x, core), gy: 16 (over z, y).
Axes of the slice: x: 4, y: 4, z: 4, core: 2. Of those that a mesh axis runs over, the one named last changes fastest.
Arguments:
- blade_state: float32 [5, 8, 524288], P(None, 'gx', 'gy'), may hold values from -6 to 6
- back_state: float32 [5, 128, 8192], P(None, 'gx', 'gy'), may hold values from -6 to 6
- blade_cotangent: float32 [5, 8, 524288], P(None, 'gx', 'gy'), may hold values from -6 to 6
- back_cotangent: float32 [5, 128, 8192], P(None, 'gx', 'gy'), may hold values from -6 to 6
- blade_flux: float32 [3, 5, 5], replicated, may hold values from -3 to 3
- back_flux: float32 [3, 5, 5], replicated, may hold values from -3 to 3
- blade_owner: int32 [2, 131072, 1], P(None, ('gx', 'gy')), may hold values from 0 to 127; in each aligned block of 1024 rows (0 to 1023, 1024 to 2047, ..., all dimensions but the last counted through in order) at most 16 rows name the same one
- back_donor_cell: int32 [2, 262144], P(None, ('gx', 'gy')), may hold values from 32 to 7614, as said below
- back_donor_weight: float32 [2, 8, 262144], P(None, None, ('gx', 'gy')), may hold values from 0 to 1, as said below
- hole_cell: int32 [2, 262144], P(None, ('gx', 'gy')), may hold values from 0 to 8159, as said below
- hole_owner: int32 [2, 262144, 1], P(None, ('gx', 'gy')), may hold values from 0 to 127; in each aligned block of 2048 rows (0 to 2047, 2048 to 4095, ..., all dimensions but the last counted through in order) at most 32 rows name the same one
- blade_donor_cell: int32 [2, 524288], P(None, ('gx', 'gy')), may hold values from 0 to 24190, as said below
- blade_donor_weight: float32 [2, 8, 524288], P(None, None, ('gx', 'gy')), may hold values from 0 to 1, as said below
Outputs:
- blade_adjoint: float32 [5, 8, 524288], P(None, 'gx', 'gy')
- back_adjoint: float32 [5, 128, 8192], P(None, 'gx', 'gy')
Inputs may be any that keep to these rules, and one draw needn't show every extreme that they name: `blade_owner`: in each step, at most 16 rim receivers of one device name the same owner. `hole_owner`: in each step, at most 32 hole receivers of one device name the same owner. `back_donor_cell`: local cell number (x * 8 + y) * 64 + z of the owner's block with x < 15, y < 7 and 32 <= z < 63. `blade_donor_cell`: local cell number (j * 64 + k) * 128 + i of the owner's blade block with j < 3, k < 61 and i < 127. `hole_cell`: in each step the 2048 cells of one device are distinct local cell numbers (x * 8 + y) * 64 + z of that device with z < 32. `back_donor_weight`: trilinear weights: products of three fractions, nonnegative, summing to one over the 8 corners of each slot. `blade_donor_weight`: trilinear weights: products of three fractions, nonnegative, summing to one over the 8 corners of each slot.
All inputs are finite; a program needn't handle non-finite values.
Results may differ from a plain program's by a relative error of at most 0.0003.
Values sent between devices are 32-bit elements; how exact they have to be, the bound alone decides.
No kernel may reach another device: no remote copies, remote signals or barrier semaphores. Data moves between devices by JAX's collectives and lax.ppermute only.
A program may use at most 384 MiB of HBM per device.

v0:
```python
import jax
import jax.numpy as jnp
from jax import lax
from jax.experimental import pallas as pl
from jax.experimental.pallas import tpu as pltpu
from jax.sharding import PartitionSpec as P


DEVS = 128
WRAP = 4
WALL = 64
CHORD = 128
EAST = 16
NORTH = 8
VERT = 64
HALF = VERT // 2
RIMS = 1024
HOLES = 2048
QR = 2 * RIMS // DEVS
QH = 2 * HOLES // DEVS
FIELDS = 17

time_step = 0.2
damping = 0.1

F32 = jnp.float32
BF16 = jnp.bfloat16


def split(x):
    hi = x.astype(BF16)
    return hi, (x - hi.astype(F32)).astype(BF16)


def dot_nn(a, b):
    return lax.dot_general(a, b, (((1,), (0,)), ((), ())), preferred_element_type=F32)


def dot_nt(a, b):
    return lax.dot_general(a, b, (((1,), (1,)), ((), ())), preferred_element_type=F32)


def iota(shape, dim):
    return lax.broadcasted_iota(jnp.int32, shape, dim)


def one_hot(rows, index):
    return jnp.where(iota((rows, index.shape[1]), 0) == index, 1.0, 0.0)


def pair_hot(rows, index, first, second):
    position = iota((rows, index.shape[1]), 0)
    return jnp.where(position == index, first, jnp.where(position == index + 1, second, 0.0))


def lane_roll(x, amount):
    amount = amount % x.shape[-1]
    return pltpu.roll(x, amount, x.ndim - 1) if amount else x


def to_planes(block):
    rows = [block[:, y * VERT : (y + 1) * VERT] for y in range(NORTH)]
    return jnp.concatenate(rows, axis=0).T


def from_planes(field):
    turned = field.T
    return [turned[y * EAST : (y + 1) * EAST, :] for y in range(NORTH)]


def donor_parts(weights):
    w = [weights[corner : corner + 1, :] for corner in range(8)]
    x0 = (w[0] + w[1]) + (w[2] + w[3])
    x1 = (w[4] + w[5]) + (w[6] + w[7])
    y0 = (w[0] + w[1]) + (w[4] + w[5])
    y1 = (w[2] + w[3]) + (w[6] + w[7])
    z0 = (w[0] + w[2]) + (w[4] + w[6])
    z1 = (w[1] + w[3]) + (w[5] + w[7])
    return x0, x1, y0, y1, z0, z1


def short_marks(size, index):
    position = iota((size, index.shape[1]), 0).astype(jnp.int16)
    return position == index.astype(jnp.int16), position == (index + 1).astype(jnp.int16)


def pair_split(marks, first, second):
    (first_hi, first_lo), (second_hi, second_lo) = split(first), split(second)
    zero = jnp.zeros((), BF16)

    def place(a, b):
        return jnp.where(marks[0], a, jnp.where(marks[1], b, zero))

    return place(first_hi, second_hi), place(first_lo, second_lo)


def donor_rows(outer, outer_index, outer_pair, inner, inner_index, inner_pair):
    hot = pair_hot(outer, outer_index, *outer_pair)
    marks = short_marks(inner, inner_index)
    parts = [
        pair_split(marks, hot[n : n + 1, :] * inner_pair[0], hot[n : n + 1, :] * inner_pair[1])
        for n in range(outer)
    ]
    return tuple(jnp.concatenate([p[k] for p in parts], axis=0) for k in range(2))


def blade_donors(base, weights):
    x0, x1, y0, y1, z0, z1 = donor_parts(weights)
    wall = (base >> 7) & (WALL - 1)
    rows = donor_rows(WRAP, base >> 13, (x0, x1), WALL, wall, (y0, y1))
    return rows, (CHORD, base & (CHORD - 1), z0, z1)


def back_donors(base, weights):
    x0, x1, y0, y1, z0, z1 = donor_parts(weights)
    north = (base >> 6) & (NORTH - 1)
    rows = donor_rows(NORTH, north, (y0, y1), EAST, base >> 9, (x0, x1))
    return rows, (HALF, (base & (VERT - 1)) - HALF, z0, z1)


def triple_rows(rows):
    hi, lo = rows
    return jnp.concatenate([hi, lo, hi], axis=0)


def triple_lanes(rows):
    hi, lo = rows
    return jnp.concatenate([hi, hi, lo], axis=1)


def store_parts(target, place, size, field):
    hi, lo = split(field)
    rows = slice(place, place + size)
    target[rows, :] = jnp.concatenate([hi, hi, lo], axis=1)


def picked(parts, rows, cols):
    size = cols[0]
    hot = pair_hot(*cols)
    table = dot_nn(parts[...], triple_rows(rows))
    return [
        jnp.sum(table[c * size : (c + 1) * size] * hot, axis=0, keepdims=True) for c in range(5)
    ]


def spread_terms(rows, cols, mu):
    size, index, first, second = cols
    pairs = [(first * mu[c], second * mu[c]) for c in range(5)]
    tiles = {c: [] for c in range(5)}
    for start in range(0, size, 16):
        marks = short_marks(16, index - start)
        for c in range(5):
            tiles[c].append(pair_split(marks, *pairs[c]))
    hi, lo = (
        jnp.concatenate([t[k] for c in range(5) for t in tiles[c]], axis=0) for k in range(2)
    )
    return dot_nt(jnp.concatenate([hi, lo, hi], axis=1), triple_lanes(rows))


def doubled(field):
    hi, lo = split(field)
    return jnp.concatenate([hi, lo], axis=1)


def twice(marks):
    return jnp.concatenate([marks, marks], axis=0)


def wall_shift(v, up):
    position = iota(v.shape, 0)
    if up:
        return jnp.where(position == v.shape[0] - 1, 0.0, pltpu.roll(v, v.shape[0] - 1, 0))
    return jnp.where(position == 0, 0.0, pltpu.roll(v, 1, 0))


def lane_shift(v, up, width, period, fill):
    place = (iota(v.shape, 1) // width) % period
    if up:
        return jnp.where(place == period - 1, fill, lane_roll(v, -width))
    return jnp.where(place == 0, fill, lane_roll(v, width))


class Matrices:
    def __init__(self, ref, start):
        self.ref, self.start = ref, start

    def __getitem__(self, place):
        return self.ref[self.start + place[0], place[1]]


def flux_of(m_ref, t, v, scaled):
    out = []
    for c in range(5):
        total = v[1 + t] * scaled[c]
        for e in range(5):
            total = total + m_ref[t, c * 5 + e] * scaled[e]
        out.append(total)
    return out


def turned_of(m_ref, t, w):
    out = []
    for c in range(5):
        total = m_ref[t, c] * w[0]
        for e in range(1, 5):
            total = total + m_ref[t, e * 5 + c] * w[e]
        out.append(total)
    return out


PAIRS = [(0, 1), (0, 2), (0, 3), (4, 1), (4, 2), (4, 3), (1, 1), (1, 2), (1, 3), (2, 2), (2, 3), (3, 3)]


def linear_fields(m_ref, center, sides):
    base = [center[c] * (1.0 - 6.0 * damping * time_step) for c in range(5)]
    jumps = []
    for t, (upper, lower) in enumerate(sides):
        jump = [0.5 * time_step * (lower[c] - upper[c]) for c in range(5)]
        turned = turned_of(m_ref, t, jump)
        for c in range(5):
            base[c] = base[c] - turned[c] + damping * time_step * (upper[c] + lower[c])
        jumps.append(jump)
    out = list(base)
    for a, b in PAIRS:
        if a in (0, 4):
            out.append(jumps[b - 1][a])
        else:
            out.append(jumps[a - 1][b] + jumps[b - 1][a])
    return out


def apply_fields(fields, v):
    out = []
    table = {pair: 5 + n for n, pair in enumerate(PAIRS)}
    for c in range(5):
        total = fields[c]
        for e in range(5):
            key = (c, e) if (c, e) in table else (e, c)
            if key in table:
                total = total - fields[table[key]] * v[e]
        out.append(total)
    return out


def adjoint_at(m_ref, v, center, sides):
    out = [center[c] * (1.0 - 6.0 * damping * time_step) for c in range(5)]
    for t, (upper, lower) in enumerate(sides):
        jump = [0.5 * time_step * (lower[c] - upper[c]) for c in range(5)]
        turned = turned_of(m_ref, t, jump)
        inner = v[0] * jump[0]
        for e in range(1, 5):
            inner = inner + v[e] * jump[e]
        for c in range(5):
            total = turned[c] + v[1 + t] * jump[c]
            if c == 1 + t:
                total = total + inner
            out[c] = out[c] - total + damping * time_step * (upper[c] + lower[c])
    return out


def blade_sides(ref, low, high, j):
    def plane(n):
        if n < 0 or n >= WRAP:
            return low if n < 0 else high
        return [ref[c, n * WALL : (n + 1) * WALL, :] for c in range(5)]

    center, above, below = plane(j), plane(j + 1), plane(j - 1)
    wall = ([wall_shift(v, True) for v in center], [wall_shift(v, False) for v in center])
    span = (
        [lane_shift(v, True, 1, CHORD, 0.0) for v in center],
        [lane_shift(v, False, 1, CHORD, 0.0) for v in center],
    )
    return center, [(above, below), wall, span]


def back_sides(center, halo):
    east = (
        [lane_shift(v, True, 1, EAST, halo[1][c]) for c, v in enumerate(center)],
        [lane_shift(v, False, 1, EAST, halo[0][c]) for c, v in enumerate(center)],
    )
    north = (
        [lane_shift(v, True, EAST, NORTH, halo[3][c]) for c, v in enumerate(center)],
        [lane_shift(v, False, EAST, NORTH, halo[2][c]) for c, v in enumerate(center)],
    )
    vert = ([wall_shift(v, True) for v in center], [wall_shift(v, False) for v in center])
    return [east, north, vert]


def pack_east(v, x):
    lane = iota((8, DEVS), 1)
    out = jnp.zeros((8, DEVS), F32)
    for g in range(8):
        out = jnp.where(lane % EAST == g, lane_roll(v[g * 8 : g * 8 + 8, :], g - x), out)
    return out


def unpack_east(v, x):
    return jnp.concatenate([lane_roll(v, x - g) for g in range(8)], axis=0)


def pack_north(v, y):
    lane = iota((8, DEVS), 1)
    out = jnp.zeros((8, DEVS), F32)
    for g in range(8):
        out = jnp.where(lane // EAST == g, lane_roll(v[g * 8 : g * 8 + 8, :], (g - y) * EAST), out)
    return out


def unpack_north(v, y):
    return jnp.concatenate([lane_roll(v, (y - g) * EAST) for g in range(8)], axis=0)


def store_blade_edges(planes, rows, edges, at=0):
    even_y = lax.axis_index("gy") % 2 == 0
    first_y, second_y = edges
    count = rows.stop - rows.start
    for c in range(5):
        low, high = (plane[c, rows, :] for plane in planes)
        first_y[c, at : at + count, :] = jnp.where(even_y, high, low)
        second_y[c, at : at + count, :] = jnp.where(even_y, low, high)


def store_back_edges(back, edges, at):
    first_y, second_y, first_x, second_x = edges
    even_y = lax.axis_index("gy") % 2 == 0
    even_x = lax.axis_index("gx") % 2 == 0
    for c in range(5):
        high, low = pack_north(back[c], NORTH - 1), pack_north(back[c], 0)
        first_y[c, at : at + 8, :] = jnp.where(even_y, high, low)
        second_y[c, at : at + 8, :] = jnp.where(even_y, low, high)
        high, low = pack_east(back[c], EAST - 1), pack_east(back[c], 0)
        first_x[c] = jnp.where(even_x, high, low)
        second_x[c] = jnp.where(even_x, low, high)


def edge_shapes(rows):
    ends = jax.ShapeDtypeStruct((5, rows, CHORD), F32)
    sides = jax.ShapeDtypeStruct((5, 8, DEVS), F32)
    return [ends, ends, sides, sides]


def read_ends(first_y, second_y, rows):
    even_y = lax.axis_index("gy") % 2 == 0
    both = [(first_y[c, rows, :], second_y[c, rows, :]) for c in range(5)]
    return [jnp.where(even_y, b, a) for a, b in both], [jnp.where(even_y, a, b) for a, b in both]


def read_back(first_y, second_y, first_x, second_x, at):
    north = lax.axis_index("gy")
    even_x = lax.axis_index("gx") % 2 == 0
    keep_low = jnp.where(north > 0, 1.0, 0.0)
    keep_high = jnp.where(north < DEVS // 8 - 1, 1.0, 0.0)
    below, above = read_ends(first_y, second_y, slice(at, at + 8))
    both = [(first_x[c], second_x[c]) for c in range(5)]
    east = [unpack_east(jnp.where(even_x, a, b), EAST - 1) for a, b in both]
    west = [unpack_east(jnp.where(even_x, b, a), 0) for a, b in both]
    south = [unpack_north(v * keep_low, 0) for v in below]
    upper = [unpack_north(v * keep_high, NORTH - 1) for v in above]
    return [west, east, south, upper]


def exchange(edges):
    gx, gy = lax.axis_size("gx"), lax.axis_size("gy")

    def pairs(start, stop, count):
        there = [(i, (i + 1) % count) for i in range(start, stop, 2)]
        return there + [(b, a) for a, b in there]

    first_y, second_y, first_x, second_x = edges
    got_y = lax.ppermute(first_y, "gy", pairs(0, gy, gy))
    got_x = lax.ppermute(first_x, "gx", pairs(0, gx, gx))
    got_x2 = lax.ppermute(second_x, "gx", pairs(1, gx - 1, gx))
    got_y2 = lax.ppermute(second_y, "gy", pairs(1, gy, gy))
    return got_y, got_y2, got_x, got_x2


def regroup(pieces, width):
    count = DEVS // width
    shape = next(piece.shape for piece in pieces if piece is not None)
    block = iota(shape, 1) // width
    out = []
    for b in range(count):
        total = jnp.zeros(shape, F32)
        for a in range(count):
            if pieces[a] is not None:
                total = jnp.where(block == a, lane_roll(pieces[a], (a - b) * width), total)
        out.append(total)
    return out


def ranks_of(owner_ref, out_ref):
    count = owner_ref.shape[1]
    earlier = jnp.where(iota((256, 256), 0) < iota((256, 256), 1), 1.0, 0.0).astype(BF16)
    carry = jnp.zeros((DEVS, 1), F32)
    for start in range(0, count, 256):
        marks = one_hot(DEVS, owner_ref[:, start : start + 256])
        before = dot_nn(marks.astype(BF16), earlier) + carry
        out_ref[:, start : start + 256] = jnp.sum(marks * before, axis=0, keepdims=True).astype(
            jnp.int32
        )
        carry = carry + jnp.sum(marks, axis=1, keepdims=True)


def seat_terms(slots, index, values):
    here = iota((slots, index.shape[1]), 0).astype(jnp.int16) == index.astype(jnp.int16)
    zero = jnp.zeros((), BF16)
    parts = [[jnp.where(here, part, zero) for part in split(v)] for v in values]
    hi, lo = (jnp.concatenate([p[k] for p in parts], axis=0) for k in range(2))
    return jnp.concatenate([hi, lo], axis=1)


def send_rows(values, owner, rank, slots):
    marks = one_hot(DEVS, owner).astype(BF16)
    return dot_nt(seat_terms(slots, rank, values), jnp.concatenate([marks, marks], axis=1))


def hole_parts(cell):
    row = ((cell >> 6) & (NORTH - 1)) * EAST + (cell >> 9)
    return row, cell & (VERT - 1)


def hole_values(low_half, cell):
    row, vert = hole_parts(cell)
    seats = one_hot(HALF, vert)
    table = dot_nn(low_half, twice(one_hot(DEVS, row).astype(BF16)))
    return [
        jnp.sum(table[n : n + HALF] * seats, axis=0, keepdims=True)
        for n in range(0, table.shape[0], HALF)
    ]


def hole_mask(cell_ref):
    total = jnp.zeros((HALF, DEVS), F32)
    for start in range(0, HOLES, 512):
        row, vert = hole_parts(cell_ref[:, start : start + 512])
        total = total + dot_nt(one_hot(HALF, vert).astype(BF16), one_hot(DEVS, row).astype(BF16))
    return total


CHUNK = 512


def chunk_lanes(n):
    return pl.ds(pl.multiple_of(n * CHUNK, CHUNK), CHUNK)


def lanes_of(ref, n, k):
    count = CHUNK // DEVS
    return jnp.concatenate([ref[k, pl.ds(n * count + m, 1), :] for m in range(count)], axis=1)


def store_chunk(out, n, values):
    for c in range(5):
        for m in range(CHUNK // DEVS):
            row = pl.ds(n * (CHUNK // DEVS) + m, 1)
            out[c, row, :] = values[c][:, m * DEVS : (m + 1) * DEVS]


def outer_planes(ref):
    return ref.at[:, :WALL, :], ref.at[:, (WRAP - 1) * WALL :, :]


def edge_kernel(
    blade_low, blade_high, cot_low, cot_high, back_cot,
    cot_planes, first_y, second_y, first_x, second_x,
):
    cots = []
    for c in range(5):
        turned = to_planes(back_cot[c])
        cot_planes[c] = turned
        cots.append(turned)
    store_blade_edges((cot_low, cot_high), slice(0, WALL), (first_y, second_y))
    store_blade_edges((blade_low, blade_high), slice(0, WALL - 8), (first_y, second_y), WALL + 8)
    store_back_edges(cots, (first_y, second_y, first_x, second_x), WALL)


def start_kernel(
    blade, back, back_base, back_weight, blade_base, blade_weight,
    send, back_planes,
    blade_parts, back_parts, hole_vals, rim_vals,
):
    for c in range(5):
        store_parts(blade_parts, c * CHORD, CHORD, blade[c].T)
        field = to_planes(back[c])
        back_planes[c] = field
        store_parts(back_parts, c * HALF, HALF, field[HALF:, :])

    def blade_step(n, carry):
        lanes = chunk_lanes(n)
        rows, cols = blade_donors(blade_base[0:1, lanes], blade_weight[0, :, lanes])
        store_chunk(hole_vals, n, picked(blade_parts, rows, cols))
        return carry

    lax.fori_loop(0, 2 * HOLES // CHUNK, blade_step, 0, unroll=4)

    def back_step(n, carry):
        lanes = chunk_lanes(n)
        rows, cols = back_donors(back_base[0:1, lanes], back_weight[0, :, lanes])
        store_chunk(rim_vals, n, picked(back_parts, rows, cols))
        return carry

    lax.fori_loop(0, 2 * RIMS // CHUNK, back_step, 0)
    store_slots(hole_vals, rim_vals, send)


def store_slots(hole_vals, rim_vals, send):
    first = regroup([hole_vals[c] for c in range(4)], QH)
    fifth = hole_vals[4]
    tail = regroup([fifth, None, None, None], QH)
    for d in range(DEVS // QH):
        send[pl.ds(d, QH, stride=DEVS // QH), 0, :] = first[d]
        send[pl.ds(d, QH, stride=DEVS // QH), 1, :] = tail[d]
    rims = regroup([None, None] + [rim_vals[c] for c in range(5)] + [None], QR)
    lane = iota((QR, DEVS), 1)
    for d in range(DEVS // QR):
        rows = pl.ds(d, QR, stride=DEVS // QR)
        send[rows, 1, :] = jnp.where(lane < QH, send[rows, 1, :], rims[d])


def cot_kernel(
    matrices, cot, cot_planes, got_y, got_y2, got_x, got_x2, rim_owner, hole_owner, hole_cell,
    send, blade_fields, back_fields, rim_rank, hole_rank,
):
    blade_m, back_m = Matrices(matrices, 0), Matrices(matrices, 3)
    low, high = read_ends(got_y, got_y2, slice(0, WALL))
    halo = read_back(got_y, got_y2, got_x, got_x2, WALL)
    for j in range(WRAP):
        center, sides = blade_sides(cot, low, high, j)
        fields = linear_fields(blade_m, center, sides)
        for n in range(FIELDS):
            blade_fields[n, j * WALL : (j + 1) * WALL, :] = fields[n]
    center = [cot_planes[c] for c in range(5)]
    fields = linear_fields(back_m, center, back_sides(center, halo))
    for n in range(FIELDS):
        back_fields[n] = fields[n]
    for step in range(2):
        ranks_of(rim_owner.at[step], rim_rank.at[step])
        ranks_of(hole_owner.at[step], hole_rank.at[step])

    total = jnp.zeros((FIELDS * QR, DEVS), F32)
    for j in range(WRAP):
        lanes = slice(j * 256, j * 256 + 256)
        top = j * WALL + WALL - 2
        values = [
            jnp.concatenate(
                [blade_fields[n, top + k : top + k + 1, :] for k in range(2)], axis=1
            )
            for n in range(FIELDS)
        ]
        total = total + send_rows(values, rim_owner[1, :, lanes], rim_rank[1, :, lanes], QR)
    total = jnp.concatenate([total, jnp.zeros((112, DEVS), F32)], axis=0)
    for m in range(3):
        send[:, 5 + m, :] = total[m * DEVS : (m + 1) * DEVS].T
    total = jnp.zeros((FIELDS * QH, DEVS), F32)
    low_half = doubled(jnp.concatenate([back_fields[n, :HALF, :] for n in range(FIELDS)], axis=0))
    for start in range(0, HOLES, 512):
        lanes = slice(start, start + 512)
        values = hole_values(low_half, hole_cell[1:2, lanes])
        total = total + send_rows(values, hole_owner[1, :, lanes], hole_rank[1, :, lanes], QH)
    total = jnp.concatenate([total, jnp.zeros((96, DEVS), F32)], axis=0)
    for m in range(5):
        send[:, m, :] = total[m * DEVS : (m + 1) * DEVS].T


def fill_kernel(
    blade, back_planes, recv, rim_owner, hole_owner, rim_rank, hole_rank, hole_cell,
    blade_first, back_first, first_y, second_y, first_x, second_x,
):
    arrived = doubled(jnp.concatenate([recv[:, 0, :].T, recv[:, 1, :].T], axis=0))
    for c in range(5):
        for j in range(WRAP):
            rows = slice(j * WALL, (j + 1) * WALL)
            blade_first[c, rows, :] = blade[c, rows, :]
    base = 5 * QH
    for j in range(WRAP):
        lanes = slice(j * 256, j * 256 + 256)
        marks = one_hot(DEVS, rim_owner[0, :, lanes]).astype(BF16)
        seats = one_hot(QR, rim_rank[0, :, lanes])
        table = dot_nn(arrived[base : base + 5 * QR], twice(marks))
        for c in range(5):
            value = jnp.sum(table[c * QR : (c + 1) * QR] * seats, axis=0, keepdims=True)
            for k in range(2):
                row = j * WALL + WALL - 2 + k
                blade_first[c, row : row + 1, :] = value[:, k * CHORD : (k + 1) * CHORD]
    filled = jnp.zeros((6 * HALF, DEVS), F32)
    for start in range(0, HOLES, 512):
        lanes = slice(start, start + 512)
        marks = one_hot(DEVS, hole_owner[0, :, lanes]).astype(BF16)
        seats = one_hot(QH, hole_rank[0, :, lanes])
        row, vert = hole_parts(hole_cell[0:1, lanes])
        table = dot_nn(arrived[:base], twice(marks))
        values = [
            jnp.sum(table[c * QH : (c + 1) * QH] * seats, axis=0, keepdims=True) for c in range(5)
        ]
        terms = seat_terms(HALF, vert, values + [jnp.ones(vert.shape, F32)])
        row_marks = one_hot(DEVS, row).astype(BF16)
        filled = filled + dot_nt(terms, jnp.concatenate([row_marks, row_marks], axis=1))
    mask = filled[5 * HALF :]
    backs = []
    for c in range(5):
        top = jnp.where(mask > 0.5, filled[c * HALF : (c + 1) * HALF], back_planes[c, :HALF, :])
        field = jnp.concatenate([top, back_planes[c, HALF:, :]], axis=0)
        back_first[c] = field
        backs.append(field)
    store_blade_edges(outer_planes(blade_first), slice(WALL - 8, WALL), (first_y, second_y))
    store_back_edges(backs, (first_y, second_y, first_x, second_x), 8)


def residual_step(center, halo_flux):
    out = [center[c] * (1.0 - 6.0 * damping * time_step) for c in range(5)]
    for t in range(3):
        upper, lower = halo_flux(t)
        for c in range(5):
            out[c] = out[c] - upper[c] + lower[c]
    return out


def side_terms(m_ref, t, v):
    flux = flux_of(m_ref, t, v, [0.5 * time_step * v[c] for c in range(5)])
    damped = [damping * time_step * v[c] for c in range(5)]
    upper = [flux[c] - damped[c] for c in range(5)]
    lower = [flux[c] + damped[c] for c in range(5)]
    return upper, lower


def middle_kernel(
    matrices, blade_first, back_first, old_y, old_y2, got_y, got_y2, got_x, got_x2,
    blade_fields, back_fields, recv, back_base, back_weight, blade_base, blade_weight, hole_cell,
    blade_mid, back_mid, first_y, second_y, first_x, second_x,
    blade_next, back_next, blade_parts, back_parts, hole_lin, rim_lin, blade_acc, back_acc,
):
    blade_m, back_m = Matrices(matrices, 0), Matrices(matrices, 3)
    planes = zip(
        read_ends(old_y, old_y2, slice(WALL + 8, 2 * WALL)), read_ends(got_y, got_y2, slice(0, 8))
    )
    low, high = (
        [jnp.concatenate([a, b], axis=0) for a, b in zip(inner, outer)] for inner, outer in planes
    )
    halo = read_back(got_y, got_y2, got_x, got_x2, 8)

    sections = [low]
    for j in range(WRAP):
        sections.append([blade_first[c, j * WALL : (j + 1) * WALL, :] for c in range(5)])
    sections.append(high)
    turns = [side_terms(blade_m, 0, plane) for plane in sections]
    for j in range(WRAP):
        center = sections[j + 1]

        def around(t, j=j, center=center):
            if t == 0:
                return turns[j + 2][0], turns[j][1]
            upper, lower = side_terms(blade_m, t, center)
            if t == 1:
                return [wall_shift(v, True) for v in upper], [wall_shift(v, False) for v in lower]
            return (
                [lane_shift(v, True, 1, CHORD, 0.0) for v in upper],
                [lane_shift(v, False, 1, CHORD, 0.0) for v in lower],
            )

        out = residual_step(center, around)
        for c in range(5):
            blade_next[c, j * WALL : (j + 1) * WALL, :] = out[c]
    center = [back_first[c] for c in range(5)]

    def across(t):
        upper, lower = side_terms(back_m, t, center)
        if t == 2:
            return [wall_shift(v, True) for v in upper], [wall_shift(v, False) for v in lower]
        width, period = ((1, EAST), (EAST, NORTH))[t]
        below = side_terms(back_m, t, halo[2 * t])[1]
        above = side_terms(back_m, t, halo[2 * t + 1])[0]
        return (
            [lane_shift(upper[c], True, width, period, above[c]) for c in range(5)],
            [lane_shift(lower[c], False, width, period, below[c]) for c in range(5)],
        )

    out = residual_step(center, across)
    for c in range(5):
        back_next[c] = out[c]
        store_parts(back_parts, c * HALF, HALF, out[c][HALF:, :])
        store_parts(blade_parts, c * CHORD, CHORD, blade_next[c].T)

    for j in range(WRAP):
        rows = slice(j * WALL, (j + 1) * WALL)
        v = [blade_next[c, rows, :] for c in range(5)]
        own = apply_fields([blade_fields[n, rows, :] for n in range(FIELDS)], v)
        inside = iota((WALL, CHORD), 0) < WALL - 2
        for c in range(5):
            blade_mid[c, rows, :] = jnp.where(inside, own[c], 0.0)
    mask = hole_mask(hole_cell.at[1:2])
    own = apply_fields([back_fields[n] for n in range(FIELDS)], [back_next[c] for c in range(5)])
    for c in range(5):
        back_mid[c, :HALF, :] = jnp.where(mask > 0.5, 0.0, own[c][:HALF, :])
        back_mid[c, HALF:, :] = own[c][HALF:, :]

    for m in range(5):
        pieces = [recv[pl.ds(d, QH, stride=DEVS // QH), m, :] for d in range(DEVS // QH)]
        for b, piece in enumerate(regroup(pieces, QH)):
            if m * 4 + b < FIELDS:
                hole_lin[m * 4 + b] = piece
    for m in range(3):
        pieces = [recv[pl.ds(d, QR, stride=DEVS // QR), 5 + m, :] for d in range(DEVS // QR)]
        for b, piece in enumerate(regroup(pieces, QR)):
            if m * 8 + b < FIELDS:
                rim_lin[m * 8 + b] = piece

    blade_acc[...] = jnp.zeros(blade_acc.shape, F32)
    back_acc[...] = jnp.zeros(back_acc.shape, F32)

    def blade_step(n, carry):
        lanes = chunk_lanes(n)
        rows, cols = blade_donors(blade_base[1:2, lanes], blade_weight[1, :, lanes])
        value = picked(blade_parts, rows, cols)
        mu = apply_fields([lanes_of(hole_lin, n, k) for k in range(FIELDS)], value)
        blade_acc[...] += spread_terms(rows, cols, mu)
        return carry

    lax.fori_loop(0, 2 * HOLES // CHUNK, blade_step, 0, unroll=4)

    def back_step(n, carry):
        lanes = chunk_lanes(n)
        rows, cols = back_donors(back_base[1:2, lanes], back_weight[1, :, lanes])
        value = picked(back_parts, rows, cols)
        mu = apply_fields([lanes_of(rim_lin, n, k) for k in range(FIELDS)], value)
        back_acc[...] += spread_terms(rows, cols, mu)
        return carry

    lax.fori_loop(0, 2 * RIMS // CHUNK, back_step, 0)
    for c in range(5):
        blade_mid[c] = blade_mid[c] + blade_acc[c * CHORD : (c + 1) * CHORD, :].T
        back_mid[c, HALF:, :] = back_mid[c, HALF:, :] + back_acc[c * HALF : (c + 1) * HALF, :]
    store_blade_edges(outer_planes(blade_mid), slice(0, WALL), (first_y, second_y))
    store_back_edges(
        [back_mid[c] for c in range(5)], (first_y, second_y, first_x, second_x), WALL
    )


def inner_kernel(
    matrices, blade_first, back_first, blade_mid, back_mid, hole_cell, blade_part, back_part, mask
):
    blade_m, back_m = Matrices(matrices, 0), Matrices(matrices, 3)
    nothing = [jnp.zeros((WALL, CHORD), F32)] * 5
    for j in range(WRAP):
        rows = slice(j * WALL, (j + 1) * WALL)
        center, sides = blade_sides(blade_mid, nothing, nothing, j)
        out = adjoint_at(blade_m, [blade_first[c, rows, :] for c in range(5)], center, sides)
        for c in range(5):
            blade_part[c, rows, :] = out[c]
    nothing = [jnp.zeros((VERT, DEVS), F32)] * 5
    center = [back_mid[c] for c in range(5)]
    sides = back_sides(center, [nothing] * 4)
    out = adjoint_at(back_m, [back_first[c] for c in range(5)], center, sides)
    for c in range(5):
        back_part[c] = out[c]
    mask[...] = hole_mask(hole_cell.at[0:1])


def outside_terms(m_ref, t, v, beyond, sign):
    jump = [-sign * 0.5 * time_step * beyond[c] for c in range(5)]
    turned = turned_of(m_ref, t, jump)
    inner = v[0] * jump[0]
    for e in range(1, 5):
        inner = inner + v[e] * jump[e]
    out = []
    for c in range(5):
        total = turned[c] + v[1 + t] * jump[c]
        if c == 1 + t:
            total = total + inner
        out.append(damping * time_step * beyond[c] - total)
    return out


def last_kernel(
    matrices, blade_first, back_first, blade_part, back_part, mask,
    got_y, got_y2, got_x, got_x2,
    rim_owner, hole_owner, rim_rank, hole_rank, hole_cell,
    send, blade_kept, back_kept,
):
    blade_m, back_m = Matrices(matrices, 0), Matrices(matrices, 3)
    low, high = read_ends(got_y, got_y2, slice(0, WALL))
    halo = read_back(got_y, got_y2, got_x, got_x2, WALL)
    rims = jnp.zeros((5 * QR, DEVS), F32)
    for j in range(WRAP):
        rows = slice(j * WALL, (j + 1) * WALL)
        out = [blade_part[c, rows, :] for c in range(5)]
        if j in (0, WRAP - 1):
            v = [blade_first[c, rows, :] for c in range(5)]
            beyond, sign = (high, 1.0) if j else (low, -1.0)
            more = outside_terms(blade_m, 0, v, beyond, sign)
            out = [out[c] + more[c] for c in range(5)]
        inside = iota((WALL, CHORD), 0) < WALL - 2
        values = []
        for c in range(5):
            blade_kept[c, rows, :] = jnp.where(inside, out[c], 0.0)
            outer = [out[c][WALL - 2 + k : WALL - 1 + k, :] for k in range(2)]
            values.append(jnp.concatenate(outer, axis=1))
        lanes = slice(j * 256, j * 256 + 256)
        rims = rims + send_rows(values, rim_owner[0, :, lanes], rim_rank[0, :, lanes], QR)
    v = [back_first[c] for c in range(5)]
    out = [back_part[c] for c in range(5)]
    place = iota((VERT, DEVS), 1)
    east, north = place % EAST, place // EAST
    for t, beyond, sign, at in (
        (0, halo[0], -1.0, east == 0),
        (0, halo[1], 1.0, east == EAST - 1),
        (1, halo[2], -1.0, north == 0),
        (1, halo[3], 1.0, north == NORTH - 1),
    ):
        more = outside_terms(back_m, t, v, [jnp.where(at, x, 0.0) for x in beyond], sign)
        out = [out[c] + more[c] for c in range(5)]
    holes_here = mask[...] > 0.5
    for c in range(5):
        back_kept[c, :HALF, :] = jnp.where(holes_here, 0.0, out[c][:HALF, :])
        back_kept[c, HALF:, :] = out[c][HALF:, :]
    holes = jnp.zeros((5 * QH, DEVS), F32)
    low_half = doubled(jnp.concatenate([out[c][:HALF, :] for c in range(5)], axis=0))
    for start in range(0, HOLES, 512):
        lanes = slice(start, start + 512)
        values = hole_values(low_half, hole_cell[0:1, lanes])
        holes = holes + send_rows(values, hole_owner[0, :, lanes], hole_rank[0, :, lanes], QH)
    rest = jnp.zeros((2 * DEVS - 5 * QH - 5 * QR, DEVS), F32)
    total = jnp.concatenate([holes, rims, rest], axis=0)
    send[:, 0, :] = total[:DEVS].T
    send[:, 1, :] = total[DEVS:].T


def end_kernel(
    blade_kept, back_kept, recv, back_base, back_weight, blade_base, blade_weight,
    blade_out, back_out, hole_mu, rim_mu, blade_acc, back_acc,
):
    count = DEVS // QH
    pieces = [recv[pl.ds(d, QH, stride=count), 0, :] for d in range(count)]
    for c, piece in enumerate(regroup(pieces, QH)):
        hole_mu[c] = piece
    pieces = [recv[pl.ds(d, QH, stride=count), 1, :] for d in range(count)]
    hole_mu[4] = regroup(pieces, QH)[0]
    count = DEVS // QR
    pieces = [recv[pl.ds(d, QR, stride=count), 1, :] for d in range(count)]
    groups = regroup(pieces, QR)
    for c in range(5):
        rim_mu[c] = groups[QH // QR + c]
    blade_acc[...] = jnp.zeros(blade_acc.shape, F32)
    back_acc[...] = jnp.zeros(back_acc.shape, F32)

    def blade_step(n, carry):
        lanes = chunk_lanes(n)
        rows, cols = blade_donors(blade_base[0:1, lanes], blade_weight[0, :, lanes])
        blade_acc[...] += spread_terms(rows, cols, [lanes_of(hole_mu, n, c) for c in range(5)])
        return carry

    lax.fori_loop(0, 2 * HOLES // CHUNK, blade_step, 0, unroll=4)

    def back_step(n, carry):
        lanes = chunk_lanes(n)
        rows, cols = back_donors(back_base[0:1, lanes], back_weight[0, :, lanes])
        back_acc[...] += spread_terms(rows, cols, [lanes_of(rim_mu, n, c) for c in range(5)])
        return carry

    lax.fori_loop(0, 2 * RIMS // CHUNK, back_step, 0)
    for c in range(5):
        blade_out[c] = blade_kept[c] + blade_acc[c * CHORD : (c + 1) * CHORD, :].T
        top = back_kept[c, HALF:, :] + back_acc[c * HALF : (c + 1) * HALF, :]
        parts = from_planes(jnp.concatenate([back_kept[c, :HALF, :], top], axis=0))
        for y in range(0, NORTH, 2):
            back_out[c, :, y * VERT : (y + 2) * VERT] = jnp.concatenate(parts[y : y + 2], axis=1)


VMEM = pl.BlockSpec(memory_space=pltpu.VMEM)
SMEM = pl.BlockSpec(memory_space=pltpu.SMEM)
BLADE = jax.ShapeDtypeStruct((5, WRAP * WALL, CHORD), F32)
PLANES = jax.ShapeDtypeStruct((5, VERT, DEVS), F32)
DONOR_PARTS = [
    pltpu.VMEM((5 * CHORD, 3 * WRAP * WALL), BF16),
    pltpu.VMEM((5 * HALF, 3 * DEVS), BF16),
]
SUMS = [pltpu.VMEM((5 * CHORD, WRAP * WALL), F32), pltpu.VMEM((5 * HALF, DEVS), F32)]


def plane_block(j):
    return pl.BlockSpec((5, WALL, CHORD), lambda _: (0, j, 0))


def run(kernel, args, out_shape, scratch=(), scalars=0, flops=0, blocks=None):
    size = sum(4 * a.size for a in args) + sum(4 * o.size for o in out_shape)
    return pl.pallas_call(
        kernel,
        grid=(1,) if blocks else (),
        out_shape=list(out_shape),
        in_specs=blocks or [SMEM] * scalars + [VMEM] * (len(args) - scalars),
        out_specs=[VMEM] * len(out_shape),
        scratch_shapes=list(scratch),
        cost_estimate=pl.CostEstimate(flops=flops, bytes_accessed=size, transcendentals=0),
    )(*args)


def swap(rows):
    return lax.all_to_all(rows, ("gx", "gy"), split_axis=0, concat_axis=0, tiled=True)


def body(
    blade_state,
    back_state,
    blade_cotangent,
    back_cotangent,
    blade_flux,
    back_flux,
    blade_owner,
    back_donor_cell,
    back_donor_weight,
    hole_cell,
    hole_owner,
    blade_donor_cell,
    blade_donor_weight,
):
    shape = jax.ShapeDtypeStruct
    blade = blade_state.reshape(5, WRAP * WALL, CHORD)
    cot = blade_cotangent.reshape(5, WRAP * WALL, CHORD)
    matrices = jnp.concatenate([blade_flux, back_flux]).reshape(6, 25)
    owners = (blade_owner.reshape(2, 1, RIMS), hole_owner.reshape(2, 1, HOLES))
    tables = (back_donor_cell, back_donor_weight, blade_donor_cell, blade_donor_weight)

    cot_planes, *edges = run(
        edge_kernel,
        (blade, blade, cot, cot, back_cotangent),
        [PLANES] + edge_shapes(2 * WALL),
        blocks=[plane_block(0), plane_block(WRAP - 1)] * 2 + [VMEM],
    )
    cot_halo = exchange(edges)
    send, back_planes = run(
        start_kernel,
        (blade, back_state) + tables,
        [shape((DEVS, 2, DEVS), F32), PLANES],
        DONOR_PARTS + [pltpu.VMEM((5, QH, DEVS), F32), pltpu.VMEM((5, QR, DEVS), F32)],
        flops=5 * 10**9,
    )
    recv = swap(send)
    lin_send, blade_fields, back_fields, rim_rank, hole_rank = run(
        cot_kernel,
        (matrices, cot, cot_planes, *cot_halo, *owners, hole_cell),
        [
            shape((DEVS, 8, DEVS), F32),
            shape((FIELDS, WRAP * WALL, CHORD), F32),
            shape((FIELDS, VERT, DEVS), F32),
            shape((2, 1, RIMS), jnp.int32),
            shape((2, 1, HOLES), jnp.int32),
        ],
        scalars=1,
        flops=2 * 10**9,
    )
    lin_recv = swap(lin_send)
    slots = (*owners, rim_rank, hole_rank, hole_cell)
    blade_first, back_first, *edges = run(
        fill_kernel,
        (blade, back_planes, recv) + slots,
        [BLADE, PLANES] + edge_shapes(16),
        flops=10**9,
    )
    first_halo = exchange(edges)
    blade_mid, back_mid, *edges = run(
        middle_kernel,
        (matrices, blade_first, back_first, *cot_halo[:2], *first_halo, blade_fields, back_fields)
        + (lin_recv,)
        + tables
        + (hole_cell,),
        [BLADE, PLANES] + edge_shapes(WALL + 8),
        [pltpu.VMEM(BLADE.shape, F32), pltpu.VMEM(PLANES.shape, F32)]
        + DONOR_PARTS
        + [pltpu.VMEM((FIELDS, QH, DEVS), F32), pltpu.VMEM((FIELDS, QR, DEVS), F32)]
        + SUMS,
        scalars=1,
        flops=10**10,
    )
    mid_halo = exchange(edges)
    parts = run(
        inner_kernel,
        (matrices, blade_first, back_first, blade_mid, back_mid, hole_cell),
        [BLADE, PLANES, shape((HALF, DEVS), F32)],
        scalars=1,
        flops=10**9,
    )
    send, blade_kept, back_kept = run(
        last_kernel,
        (matrices, blade_first, back_first, *parts, *mid_halo) + slots,
        [shape((DEVS, 2, DEVS), F32), BLADE, PLANES],
        scalars=1,
        flops=10**9,
    )
    recv = swap(send)
    blade_last, back_last = run(
        end_kernel,
        (blade_kept, back_kept, recv) + tables,
        [BLADE, shape((5, EAST, NORTH * VERT), F32)],
        [pltpu.VMEM((5, QH, DEVS), F32), pltpu.VMEM((5, QR, DEVS), F32)] + SUMS,
        flops=5 * 10**9,
    )
    return (blade_last.reshape(blade_state.shape), back_last)


def solution(mesh):
    return jax.shard_map(
        body,
        mesh=mesh,
        in_specs=(
            P(None, "gx", "gy"),
            P(None, "gx", "gy"),
            P(None, "gx", "gy"),
            P(None, "gx", "gy"),
            P(),
            P(),
            P(None, ("gx", "gy"), None),
            P(None, ("gx", "gy")),
            P(None, None, ("gx", "gy")),
            P(None, ("gx", "gy")),
            P(None, ("gx", "gy"), None),
            P(None, ("gx", "gy")),
            P(None, None, ("gx", "gy")),
        ),
        out_specs=(P(None, "gx", "gy"), P(None, "gx", "gy")),
        check_vma=False,
    )
```

profile of v0, /device:TPU:1, one launch (start us, length us, event | category | flops | bytes accessed | tf_op | source)
XLA Modules:
  0.0 128.4 jit_solution(8116592321668384519)
XLA Ops:
  0.6 2.5 %shard_map.141 = (f32[5,64,128]{2,1,0:T(8,128)}, f32[5,128,128]{2,1,0:T(8,128)}, f32[5,128,128]{2,1,0:T(8,128)}, f32[5,8,128]{2,1,0:T(8,128)}, f32[5,8,128]{2,1,0:T(8,128)}) custom-call(f32[5,256,128]{2,1,0:T(8,128)} %bitcast.8, f32[5,256,128]{2,1,0:T(8,128)} %bitcast.9, f32[5,256,128]{2,1,0:T(8,128)} %bitcast.5, f32[5,256,128]{2,1,0:T(8,128)} %bitcast.6, ...), custom_call_target="tpu_custom_call" | custom-call | bytes 3645440 | tf_op jit(solution)/shard_map/pallas_call | solution.py:885
  3.2 2.1 %collective-permute-start = (f32[5,128,128]{2,1,0:T(8,128)}, f32[5,128,128]{2,1,0:T(8,128)S(1)}, u32[]{:S(2)}, u32[]{:S(2)}) collective-permute-start(f32[5,128,128]{2,1,0:T(8,128)} %get-tuple-element.37), channel_id=1, source_target_pairs={{0,1},{2,3},{4,5},{6,7},{8,9},{10,11},{12,13},{14,15},{1,0},{3,2},... | collective-permute-start | bytes 983048 | tf_op jit(solution)/shard_map/ppermute | solution.py:370
  5.3 5.5 %collective-permute-start.1 = (f32[5,128,128]{2,1,0:T(8,128)}, f32[5,128,128]{2,1,0:T(8,128)S(1)}, u32[]{:S(2)}, u32[]{:S(2)}) collective-permute-start(f32[5,128,128]{2,1,0:T(8,128)} %get-tuple-element.38), channel_id=1, source_target_pairs={{1,2},{3,4},{5,6},{7,8},{9,10},{11,12},{13,14},{15,0},{2,1},{4,3},... | collective-permute-start | bytes 983048 | tf_op jit(solution)/shard_map/ppermute | solution.py:373
  10.7 8.5 %shard_map.140 = (f32[128,2,128]{2,1,0:T(2,128)}, f32[5,64,128]{2,1,0:T(8,128)}) custom-call(f32[5,256,128]{2,1,0:T(8,128)} %bitcast.10, f32[5,16,512]{2,1,0:T(8,128)} %back.1, s32[2,2048]{1,0:T(2,128)} %back_base.5, f32[2,8,2048]{2,1,0:T(8,128)} %back_weight.5, s32[2,4096]{1,0:T(2,128)} %blade_base.5, f32[2,8,4096]{2,1,0:T(8,128)} %blade_weight.5), custom_call_target="tpu_custom_call" | custom-call | flops 5000000000 | bytes 1556480 | tf_op jit(solution)/shard_map/pallas_call | solution.py:885
  19.2 6.5 %all-to-all-start = ((f32[128,2,128]{2,1,0:T(2,128)}), f32[128,2,128]{2,1,0:T(2,128)S(1)}, u32[]{:S(2)}, u32[]{:S(2)}) async-start(f32[128,2,128]{2,1,0:T(2,128)} %get-tuple-element.35), calls=%async_computation | async-start | bytes 262144 | tf_op jit(solution)/shard_map/all_to_all | solution.py:897
  25.8 1.1 collective-permute-start.2
  26.9 2.6 %collective-permute-start.3 = (f32[5,8,128]{2,1,0:T(8,128)S(1)}, f32[5,8,128]{2,1,0:T(8,128)S(1)}, u32[]{:S(2)}, u32[]{:S(2)}) collective-permute-start(f32[5,8,128]{2,1,0:T(8,128)S(1)} %copy-done.13), channel_id=1, source_target_pairs={{16,32},{48,64},{80,96},{32,16},{64,48},{96,80},{17,33},{49,65},{8... | collective-permute-start | bytes 61448 | tf_op jit(solution)/shard_map/ppermute | solution.py:372
  29.6 0.7 reshape.22.matrices
  30.2 0.0 collective-permute-done.2.got_x
  30.2 2.1 %collective-permute-done.3.got_x2 = f32[5,8,128]{2,1,0:T(8,128)S(1)} collective-permute-done((f32[5,8,128]{2,1,0:T(8,128)S(1)}, f32[5,8,128]{2,1,0:T(8,128)S(1)}, u32[]{:S(2)}, u32[]{:S(2)}) %collective-permute-start.3) | collective-permute-done | bytes 20512 | tf_op jit(solution)/shard_map/ppermute | solution.py:372
  32.3 0.0 collective-permute-done.got_y.old_y
  32.3 0.0 collective-permute-done.1.got_y2.old_y2
  32.3 0.6 copy-done.17
  32.9 0.1 copy-done.4
  33.1 0.1 copy-done.5
  33.2 8.0 %shard_map.142 = (f32[128,8,128]{2,1,0:T(8,128)}, f32[17,256,128]{2,1,0:T(8,128)}, f32[17,64,128]{2,1,0:T(8,128)}, s32[2,1,1024]{2,1,0:T(1,128)}, s32[2,1,2048]{2,1,0:T(1,128)}) custom-call(f32[6,25]{1,0:T(8,128)} %reshape.22.matrices, f32[5,256,128]{2,1,0:T(8,128)} %bitcast.7, f32[5,64,128]{2,1,0:T(8,128)} %get-tuple-element.36.cot_planes, ...), custom_call_target="tpu_custom_call" | custom-call | flops 2000000000 | bytes 4891224 | tf_op jit(solution)/shard_map/pallas_call | solution.py:885
  41.2 0.0 all-to-all-done.recv
  41.2 8.5 %all-to-all-start.1 = ((f32[128,8,128]{2,1,0:T(8,128)}), f32[128,8,128]{2,1,0:T(8,128)S(1)}, u32[]{:S(2)}, u32[]{:S(2)}) async-start(f32[128,8,128]{2,1,0:T(8,128)} %get-tuple-element.51), calls=%async_computation.1 | async-start | bytes 1048576 | tf_op jit(solution)/shard_map/all_to_all | solution.py:897
  49.8 3.6 %shard_map.143 = (f32[5,256,128]{2,1,0:T(8,128)}, f32[5,64,128]{2,1,0:T(8,128)}, f32[5,16,128]{2,1,0:T(8,128)}, f32[5,16,128]{2,1,0:T(8,128)}, f32[5,8,128]{2,1,0:T(8,128)}, /*index=5*/f32[5,8,128]{2,1,0:T(8,128)}) custom-call(f32[5,256,128]{2,1,0:T(8,128)} %bitcast.11, f32[5,64,128]{2,1,0:T(8,128)} %get-tuple-element.34.back_planes, ...), custom_call_target="tpu_custom_call" | custom-call | flops 1000000000 | bytes 1957888 | tf_op jit(solution)/shard_map/pallas_call | solution.py:885
  53.4 1.4 %collective-permute-start.4 = (f32[5,16,128]{2,1,0:T(8,128)}, f32[5,16,128]{2,1,0:T(8,128)S(1)}, u32[]{:S(2)}, u32[]{:S(2)}) collective-permute-start(f32[5,16,128]{2,1,0:T(8,128)} %get-tuple-element.45), channel_id=1, source_target_pairs={{0,1},{2,3},{4,5},{6,7},{8,9},{10,11},{12,13},{14,15},{1,0},{3,2},... | collective-permute-start | bytes 122888 | tf_op jit(solution)/shard_map/ppermute | solution.py:370
  54.7 4.7 %collective-permute-start.5 = (f32[5,16,128]{2,1,0:T(8,128)}, f32[5,16,128]{2,1,0:T(8,128)S(1)}, u32[]{:S(2)}, u32[]{:S(2)}) collective-permute-start(f32[5,16,128]{2,1,0:T(8,128)} %get-tuple-element.46), channel_id=1, source_target_pairs={{1,2},{3,4},{5,6},{7,8},{9,10},{11,12},{13,14},{15,0},{2,1},{4,3},... | collective-permute-start | bytes 122888 | tf_op jit(solution)/shard_map/ppermute | solution.py:373
  59.4 0.9 collective-permute-start.6
  60.4 3.0 %collective-permute-start.7 = (f32[5,8,128]{2,1,0:T(8,128)}, f32[5,8,128]{2,1,0:T(8,128)S(1)}, u32[]{:S(2)}, u32[]{:S(2)}) collective-permute-start(f32[5,8,128]{2,1,0:T(8,128)} %get-tuple-element.48), channel_id=1, source_target_pairs={{16,32},{48,64},{80,96},{32,16},{64,48},{96,80},{17,33},{49,65},{8... | collective-permute-start | bytes 61448 | tf_op jit(solution)/shard_map/ppermute | solution.py:372
  63.4 0.0 collective-permute-done.6.got_x
  63.4 2.3 %collective-permute-done.7.got_x2 = f32[5,8,128]{2,1,0:T(8,128)S(1)} collective-permute-done((f32[5,8,128]{2,1,0:T(8,128)}, f32[5,8,128]{2,1,0:T(8,128)S(1)}, u32[]{:S(2)}, u32[]{:S(2)}) %collective-permute-start.7) | collective-permute-done | bytes 20512 | tf_op jit(solution)/shard_map/ppermute | solution.py:372
  65.7 0.0 collective-permute-done.4.got_y
  65.7 0.0 collective-permute-done.5.got_y2
  65.7 0.0 all-to-all-done.1.recv
  65.7 0.5 copy-done.12
  66.3 0.0 copy-done.8
  66.3 0.0 copy-done.9
  66.3 0.2 copy-done
  66.5 21.0 %shard_map.144 = (f32[5,256,128]{2,1,0:T(8,128)}, f32[5,64,128]{2,1,0:T(8,128)}, f32[5,72,128]{2,1,0:T(8,128)}, f32[5,72,128]{2,1,0:T(8,128)}, f32[5,8,128]{2,1,0:T(8,128)}, /*index=5*/f32[5,8,128]{2,1,0:T(8,128)}) custom-call(f32[6,25]{1,0:T(8,128)} %reshape.22.matrices, f32[5,256,128]{2,1,0:T(8,128)} %get-tuple-element.43.blade_first, ...), custom_call_target="tpu_custom_call" | custom-call | flops 10000000000 | bytes 6595160 | tf_op jit(solution)/shard_map/pallas_call | solution.py:885
  87.5 0.1 collective-permute-start.8
  87.6 0.7 collective-permute-start.9
  88.2 1.6 %collective-permute-start.10 = (f32[5,8,128]{2,1,0:T(8,128)}, f32[5,8,128]{2,1,0:T(8,128)S(1)}, u32[]{:S(2)}, u32[]{:S(2)}) collective-permute-start(f32[5,8,128]{2,1,0:T(8,128)} %get-tuple-element.59), channel_id=1, source_target_pairs={{0,16},{32,48},{64,80},{96,112},{16,0},{48,32},{80,64},{112,96},{1... | collective-permute-start | bytes 61448 | tf_op jit(solution)/shard_map/ppermute | solution.py:371
  89.9 3.0 %collective-permute-start.11 = (f32[5,8,128]{2,1,0:T(8,128)}, f32[5,8,128]{2,1,0:T(8,128)S(1)}, u32[]{:S(2)}, u32[]{:S(2)}) collective-permute-start(f32[5,8,128]{2,1,0:T(8,128)} %get-tuple-element.60), channel_id=1, source_target_pairs={{16,32},{48,64},{80,96},{32,16},{64,48},{96,80},{17,33},{49,65},{8... | collective-permute-start | bytes 61448 | tf_op jit(solution)/shard_map/ppermute | solution.py:372
  92.8 4.2 %shard_map.145 = (f32[5,256,128]{2,1,0:T(8,128)}, f32[5,64,128]{2,1,0:T(8,128)}, f32[32,128]{1,0:T(8,128)}) custom-call(f32[6,25]{1,0:T(8,128)} %reshape.22.matrices, f32[5,256,128]{2,1,0:T(8,128)} %get-tuple-element.43.blade_first, f32[5,64,128]{2,1,0:T(8,128)} %get-tuple-element.44.back_first, f32[5,256,128]{2,1,0:T(8,128)} %get-tuple-element.52.blade_mid, ...), custom_call_target="tpu_custom_call" | custom-call | flops 1000000000 | bytes 2490968 | tf_op jit(solution)/shard_map/pallas_call | solution.py:885
  97.0 0.0 collective-permute-done.10.got_x
  97.1 0.0 collective-permute-done.8.got_y
  97.1 0.1 collective-permute-done.9.got_y2
  97.2 0.4 copy-done.11
  97.6 0.0 copy-done.14
  97.7 0.1 copy-done.6
  97.8 0.2 copy-done.7
  97.9 4.3 %shard_map.146 = (f32[128,2,128]{2,1,0:T(2,128)}, f32[5,256,128]{2,1,0:T(8,128)}, f32[5,64,128]{2,1,0:T(8,128)}) custom-call(f32[6,25]{1,0:T(8,128)} %reshape.22.matrices, f32[5,256,128]{2,1,0:T(8,128)} %get-tuple-element.43.blade_first, f32[5,64,128]{2,1,0:T(8,128)} %get-tuple-element.44.back_first, f32[5,256,128]{2,1,0:T(8,128)} %get-tuple-element.54.blade_part, ...), custom_call_target="tpu_custom_call" | custom-call | flops 1000000000 | bytes 3080792 | tf_op jit(solution)/shard_map/pallas_call | solution.py:885
  102.3 16.8 %all_to_all.15.recv = f32[128,2,128]{2,1,0:T(2,128)} all-to-all(f32[128,2,128]{2,1,0:T(2,128)} %get-tuple-element.63), channel_id=1, replica_groups=mesh['gx'=8,'gy'=16] {'gx','gy'}, dimensions={0} | all-to-all | bytes 262144 | tf_op jit(solution)/shard_map/all_to_all | solution.py:897
  119.1 9.3 %shard_map.147 = (f32[5,256,128]{2,1,0:T(8,128)}, f32[5,16,512]{2,1,0:T(8,128)}) custom-call(f32[5,256,128]{2,1,0:T(8,128)} %get-tuple-element.61.blade_kept, f32[5,64,128]{2,1,0:T(8,128)} %get-tuple-element.62.back_kept, f32[128,2,128]{2,1,0:T(2,128)} %all_to_all.15.recv, s32[2,2048]{1,0:T(2,128)} %back_base.5, f32[2,8,2048]{2,1,0:T(8,128)} %back_weight.5, ...), custom_call_target="tpu_custom_call" | custom-call | flops 5000000000 | bytes 2211840 | tf_op jit(solution)/shard_map/pallas_call | solution.py:885
  (28 shorter events, 0.1 us)
Async XLA Ops:
  3.2 29.1 %collective-permute-start = (f32[5,128,128]{2,1,0:T(8,128)}, f32[5,128,128]{2,1,0:T(8,128)S(1)}, u32[]{:S(2)}, u32[]{:S(2)}) collective-permute-start(f32[5,128,128]{2,1,0:T(8,128)} %get-tuple-element.37), channel_id=1, source_target_pairs={{0,1},{2,3},{4,5},{6,7},{8,9},{10,11},{12,13},{14,15},{1,0},{3,2},... | collective-permute-start | bytes 983048 | tf_op jit(solution)/shard_map/ppermute | solution.py:370
  5.3 20.5 %copy-start.15 = (f32[5,8,128]{2,1,0:T(8,128)S(1)}, f32[5,8,128]{2,1,0:T(8,128)}, u32[]{:S(2)}) copy-start(f32[5,8,128]{2,1,0:T(8,128)} %get-tuple-element.39) | copy-start | bytes 61444
  5.3 21.6 %copy-start.13 = (f32[5,8,128]{2,1,0:T(8,128)S(1)}, f32[5,8,128]{2,1,0:T(8,128)}, u32[]{:S(2)}) copy-start(f32[5,8,128]{2,1,0:T(8,128)} %get-tuple-element.40) | copy-start | bytes 61444
  5.3 24.2 %copy-start.2 = (f32[3,5,5]{2,0,1:T(4,128)S(1)}, f32[3,5,5]{2,0,1:T(4,128)}, u32[]{:S(2)}) copy-start(f32[3,5,5]{2,0,1:T(4,128)} %param.18) | copy-start | bytes 904
  5.3 24.2 %copy-start.3 = (f32[3,5,5]{2,0,1:T(4,128)S(1)}, f32[3,5,5]{2,0,1:T(4,128)}, u32[]{:S(2)}) copy-start(f32[3,5,5]{2,0,1:T(4,128)} %param.17) | copy-start | bytes 904
  5.3 27.0 %collective-permute-start.1 = (f32[5,128,128]{2,1,0:T(8,128)}, f32[5,128,128]{2,1,0:T(8,128)S(1)}, u32[]{:S(2)}, u32[]{:S(2)}) collective-permute-start(f32[5,128,128]{2,1,0:T(8,128)} %get-tuple-element.38), channel_id=1, source_target_pairs={{1,2},{3,4},{5,6},{7,8},{9,10},{11,12},{13,14},{15,0},{2,1},{4,3},... | collective-permute-start | bytes 983048 | tf_op jit(solution)/shard_map/ppermute | solution.py:373
  19.2 21.9 %all-to-all-start = ((f32[128,2,128]{2,1,0:T(2,128)}), f32[128,2,128]{2,1,0:T(2,128)S(1)}, u32[]{:S(2)}, u32[]{:S(2)}) async-start(f32[128,2,128]{2,1,0:T(2,128)} %get-tuple-element.35), calls=%async_computation | async-start | bytes 262144 | tf_op jit(solution)/shard_map/all_to_all | solution.py:897
  25.8 4.5 %collective-permute-start.2 = (f32[5,8,128]{2,1,0:T(8,128)S(1)}, f32[5,8,128]{2,1,0:T(8,128)S(1)}, u32[]{:S(2)}, u32[]{:S(2)}) collective-permute-start(f32[5,8,128]{2,1,0:T(8,128)S(1)} %copy-done.15), channel_id=1, source_target_pairs={{0,16},{32,48},{64,80},{96,112},{16,0},{48,32},{80,64},{112,96},{1... | collective-permute-start | bytes 61448 | tf_op jit(solution)/shard_map/ppermute | solution.py:371
  26.9 5.4 %collective-permute-start.3 = (f32[5,8,128]{2,1,0:T(8,128)S(1)}, f32[5,8,128]{2,1,0:T(8,128)S(1)}, u32[]{:S(2)}, u32[]{:S(2)}) collective-permute-start(f32[5,8,128]{2,1,0:T(8,128)S(1)} %copy-done.13), channel_id=1, source_target_pairs={{16,32},{48,64},{80,96},{32,16},{64,48},{96,80},{17,33},{49,65},{8... | collective-permute-start | bytes 61448 | tf_op jit(solution)/shard_map/ppermute | solution.py:372
  30.2 2.1 %copy-start.16 = (f32[5,8,128]{2,1,0:T(8,128)}, f32[5,8,128]{2,1,0:T(8,128)S(1)}, u32[]{:S(2)}) copy-start(f32[5,8,128]{2,1,0:T(8,128)S(1)} %collective-permute-done.2.got_x) | copy-start | bytes 61444
  32.3 0.6 copy-start.17
  32.3 0.7 copy-start.4
  32.3 0.8 copy-start.5
  41.2 8.6 %copy-start.1 = (f32[128,2,128]{2,1,0:T(2,128)}, f32[128,2,128]{2,1,0:T(2,128)S(1)}, u32[]{:S(2)}) copy-start(f32[128,2,128]{2,1,0:T(2,128)S(1)} %all-to-all-done.recv) | copy-start | bytes 393220
  41.2 24.5 %all-to-all-start.1 = ((f32[128,8,128]{2,1,0:T(8,128)}), f32[128,8,128]{2,1,0:T(8,128)S(1)}, u32[]{:S(2)}, u32[]{:S(2)}) async-start(f32[128,8,128]{2,1,0:T(8,128)} %get-tuple-element.51), calls=%async_computation.1 | async-start | bytes 1048576 | tf_op jit(solution)/shard_map/all_to_all | solution.py:897
  53.4 12.3 %collective-permute-start.4 = (f32[5,16,128]{2,1,0:T(8,128)}, f32[5,16,128]{2,1,0:T(8,128)S(1)}, u32[]{:S(2)}, u32[]{:S(2)}) collective-permute-start(f32[5,16,128]{2,1,0:T(8,128)} %get-tuple-element.45), channel_id=1, source_target_pairs={{0,1},{2,3},{4,5},{6,7},{8,9},{10,11},{12,13},{14,15},{1,0},{3,2},... | collective-permute-start | bytes 122888 | tf_op jit(solution)/shard_map/ppermute | solution.py:370
  54.7 11.0 %collective-permute-start.5 = (f32[5,16,128]{2,1,0:T(8,128)}, f32[5,16,128]{2,1,0:T(8,128)S(1)}, u32[]{:S(2)}, u32[]{:S(2)}) collective-permute-start(f32[5,16,128]{2,1,0:T(8,128)} %get-tuple-element.46), channel_id=1, source_target_pairs={{1,2},{3,4},{5,6},{7,8},{9,10},{11,12},{13,14},{15,0},{2,1},{4,3},... | collective-permute-start | bytes 122888 | tf_op jit(solution)/shard_map/ppermute | solution.py:373
  59.4 3.9 %collective-permute-start.6 = (f32[5,8,128]{2,1,0:T(8,128)}, f32[5,8,128]{2,1,0:T(8,128)S(1)}, u32[]{:S(2)}, u32[]{:S(2)}) collective-permute-start(f32[5,8,128]{2,1,0:T(8,128)} %get-tuple-element.47), channel_id=1, source_target_pairs={{0,16},{32,48},{64,80},{96,112},{16,0},{48,32},{80,64},{112,96},{1... | collective-permute-start | bytes 61448 | tf_op jit(solution)/shard_map/ppermute | solution.py:371
  60.4 5.3 %collective-permute-start.7 = (f32[5,8,128]{2,1,0:T(8,128)}, f32[5,8,128]{2,1,0:T(8,128)S(1)}, u32[]{:S(2)}, u32[]{:S(2)}) collective-permute-start(f32[5,8,128]{2,1,0:T(8,128)} %get-tuple-element.48), channel_id=1, source_target_pairs={{16,32},{48,64},{80,96},{32,16},{64,48},{96,80},{17,33},{49,65},{8... | collective-permute-start | bytes 61448 | tf_op jit(solution)/shard_map/ppermute | solution.py:372
  63.4 2.3 %copy-start.10 = (f32[5,8,128]{2,1,0:T(8,128)}, f32[5,8,128]{2,1,0:T(8,128)S(1)}, u32[]{:S(2)}) copy-start(f32[5,8,128]{2,1,0:T(8,128)S(1)} %collective-permute-done.6.got_x) | copy-start | bytes 61444
  65.7 0.6 copy-start.12
  65.7 0.6 copy-start.8
  65.7 0.6 copy-start.9
  65.7 0.8 copy-start
  87.5 9.6 %collective-permute-start.8 = (f32[5,72,128]{2,1,0:T(8,128)}, f32[5,72,128]{2,1,0:T(8,128)S(1)}, u32[]{:S(2)}, u32[]{:S(2)}) collective-permute-start(f32[5,72,128]{2,1,0:T(8,128)} %get-tuple-element.57), channel_id=1, source_target_pairs={{0,1},{2,3},{4,5},{6,7},{8,9},{10,11},{12,13},{14,15},{1,0},{3,2},... | collective-permute-start | bytes 552968 | tf_op jit(solution)/shard_map/ppermute | solution.py:370
  87.6 9.7 %collective-permute-start.9 = (f32[5,72,128]{2,1,0:T(8,128)}, f32[5,72,128]{2,1,0:T(8,128)S(1)}, u32[]{:S(2)}, u32[]{:S(2)}) collective-permute-start(f32[5,72,128]{2,1,0:T(8,128)} %get-tuple-element.58), channel_id=1, source_target_pairs={{1,2},{3,4},{5,6},{7,8},{9,10},{11,12},{13,14},{15,0},{2,1},{4,3},... | collective-permute-start | bytes 552968 | tf_op jit(solution)/shard_map/ppermute | solution.py:373
  88.2 8.8 %collective-permute-start.10 = (f32[5,8,128]{2,1,0:T(8,128)}, f32[5,8,128]{2,1,0:T(8,128)S(1)}, u32[]{:S(2)}, u32[]{:S(2)}) collective-permute-start(f32[5,8,128]{2,1,0:T(8,128)} %get-tuple-element.59), channel_id=1, source_target_pairs={{0,16},{32,48},{64,80},{96,112},{16,0},{48,32},{80,64},{112,96},{1... | collective-permute-start | bytes 61448 | tf_op jit(solution)/shard_map/ppermute | solution.py:371
  89.9 7.2 %collective-permute-start.11 = (f32[5,8,128]{2,1,0:T(8,128)}, f32[5,8,128]{2,1,0:T(8,128)S(1)}, u32[]{:S(2)}, u32[]{:S(2)}) collective-permute-start(f32[5,8,128]{2,1,0:T(8,128)} %get-tuple-element.60), channel_id=1, source_target_pairs={{16,32},{48,64},{80,96},{32,16},{64,48},{96,80},{17,33},{49,65},{8... | collective-permute-start | bytes 61448 | tf_op jit(solution)/shard_map/ppermute | solution.py:372
  97.0 0.6 copy-start.11
  97.1 0.6 copy-start.14
  97.1 0.7 copy-start.6
  97.2 0.7 copy-start.7
where the time goes:
time: 129 us; the launch traced here: 128 us
  Pallas kernels  61.4 us (48%)
  starting transfers between devices  41.7 us (32%)
  blocking collectives  16.8 us (13%)
  waiting for transfers between devices  4.52 us (4%)
  local copies, waits for them, and re-layouts  3 us (2%)
    pallas_call x8, Pallas kernels, run(): pl.pallas_call(kernel, grid=(1,) if blocks else (), out_shape=list(out_sh...  61.4 us
    all_to_all x1, blocking collectives, swap(): lax.all_to_all(rows, ('gx', 'gy'), split_axis=0, concat_axis=0, tiled=True)  16.8 us
    all_to_all x2, starting transfers between devices, swap(): lax.all_to_all(rows, ('gx', 'gy'), split_axis=0, concat_axis=0, tiled=True)  15.1 us
    ppermute x3, starting transfers between devices, exchange(): got_y2 = lax.ppermute(second_y, 'gy', pairs(1, gy, gy))  10.8 us
    ppermute x3, starting transfers between devices, exchange(): got_x2 = lax.ppermute(second_x, 'gx', pairs(1, gx - 1, gx))  8.55 us
    ppermute x3, waiting for transfers between devices, exchange(): got_x2 = lax.ppermute(second_x, 'gx', pairs(1, gx - 1, gx))  4.36 us
    ppermute x3, starting transfers between devices, exchange(): got_x = lax.ppermute(first_x, 'gx', pairs(0, gx, gx))  3.71 us
    ppermute x3, starting transfers between devices, exchange(): got_y = lax.ppermute(first_y, 'gy', pairs(0, gy, gy))  3.55 us
  transfers between devices with their start and end apart: 14, of which 3 were waited for; matrix products, arithmetic and copies ran while one was open for 1% of the time, Pallas kernels for 19%

commit v1 on v0

--- a/solution.py
+++ b/solution.py
@@ -499,7 +499,7 @@
         store_chunk(rim_vals, n, picked(back_parts, rows, cols))
         return carry
 
-    lax.fori_loop(0, 2 * RIMS // CHUNK, back_step, 0)
+    lax.fori_loop(0, 2 * RIMS // CHUNK, back_step, 0, unroll=2)
     store_slots(hole_vals, rim_vals, send)
 
 
@@ -725,7 +725,7 @@
         back_acc[...] += spread_terms(rows, cols, mu)
         return carry
 
-    lax.fori_loop(0, 2 * RIMS // CHUNK, back_step, 0)
+    lax.fori_loop(0, 2 * RIMS // CHUNK, back_step, 0, unroll=2)
     for c in range(5):
         blade_mid[c] = blade_mid[c] + blade_acc[c * CHORD : (c + 1) * CHORD, :].T
         back_mid[c, HALF:, :] = back_mid[c, HALF:, :] + back_acc[c * HALF : (c + 1) * HALF, :]
@@ -856,7 +856,7 @@
         back_acc[...] += spread_terms(rows, cols, [lanes_of(rim_mu, n, c) for c in range(5)])
         return carry
 
-    lax.fori_loop(0, 2 * RIMS // CHUNK, back_step, 0)
+    lax.fori_loop(0, 2 * RIMS // CHUNK, back_step, 0, unroll=2)
     for c in range(5):
         blade_out[c] = blade_kept[c] + blade_acc[c * CHORD : (c + 1) * CHORD, :].T
         top = back_kept[c, HALF:, :] + back_acc[c * HALF : (c + 1) * HALF, :]

time: 129 us -> 128 us (level)
  transfers between devices with their start and end apart: 14 -> 14, of which waited for: 3 -> 2; matrix products, arithmetic and copies ran while one was open for 1% -> 1% of each run, Pallas kernels for 19% -> 19%
where the time goes in v1:
time: 128 us; the launch traced here: 127 us
  Pallas kernels  60.2 us (47%)
  starting transfers between devices  41.9 us (33%)
  blocking collectives  16.9 us (13%)
  waiting for transfers between devices  4.39 us (3%)
  local copies, waits for them, and re-layouts  3.06 us (2%)
    pallas_call x8, Pallas kernels, run(): pl.pallas_call(kernel, grid=(1,) if blocks else (), out_shape=list(out_sh...  60.2 us
    all_to_all x1, blocking collectives, swap(): lax.all_to_all(rows, ('gx', 'gy'), split_axis=0, concat_axis=0, tiled=True)  16.9 us
    all_to_all x2, starting transfers between devices, swap(): lax.all_to_all(rows, ('gx', 'gy'), split_axis=0, concat_axis=0, tiled=True)  15.1 us
    ppermute x3, starting transfers between devices, exchange(): got_y2 = lax.ppermute(second_y, 'gy', pairs(1, gy, gy))  10.8 us
    ppermute x3, starting transfers between devices, exchange(): got_x2 = lax.ppermute(second_x, 'gx', pairs(1, gx - 1, gx))  8.55 us
    ppermute x3, waiting for transfers between devices, exchange(): got_x2 = lax.ppermute(second_x, 'gx', pairs(1, gx - 1, gx))  4.36 us
    ppermute x3, starting transfers between devices, exchange(): got_x = lax.ppermute(first_x, 'gx', pairs(0, gx, gx))  3.91 us
    ppermute x3, starting transfers between devices, exchange(): got_y = lax.ppermute(first_y, 'gy', pairs(0, gy, gy))  3.56 us
  transfers between devices with their start and end apart: 14, of which 2 were waited for; matrix products, arithmetic and copies ran while one was open for 1% of the time, Pallas kernels for 19%

profile of v1, /device:TPU:1, one launch (start us, length us, event | category | flops | bytes accessed | tf_op | source)
XLA Modules:
  0.0 127.4 jit_solution(13672786278456728711)
XLA Ops:
  0.6 2.5 %shard_map.141 = (f32[5,64,128]{2,1,0:T(8,128)}, f32[5,128,128]{2,1,0:T(8,128)}, f32[5,128,128]{2,1,0:T(8,128)}, f32[5,8,128]{2,1,0:T(8,128)}, f32[5,8,128]{2,1,0:T(8,128)}) custom-call(f32[5,256,128]{2,1,0:T(8,128)} %bitcast.8, f32[5,256,128]{2,1,0:T(8,128)} %bitcast.9, f32[5,256,128]{2,1,0:T(8,128)} %bitcast.5, f32[5,256,128]{2,1,0:T(8,128)} %bitcast.6, ...), custom_call_target="tpu_custom_call" | custom-call | bytes 3645440 | tf_op jit(solution)/shard_map/pallas_call | solution.py:885
  3.2 2.1 %collective-permute-start = (f32[5,128,128]{2,1,0:T(8,128)}, f32[5,128,128]{2,1,0:T(8,128)S(1)}, u32[]{:S(2)}, u32[]{:S(2)}) collective-permute-start(f32[5,128,128]{2,1,0:T(8,128)} %get-tuple-element.37), channel_id=1, source_target_pairs={{0,1},{2,3},{4,5},{6,7},{8,9},{10,11},{12,13},{14,15},{1,0},{3,2},... | collective-permute-start | bytes 983048 | tf_op jit(solution)/shard_map/ppermute | solution.py:370
  5.3 5.5 %collective-permute-start.1 = (f32[5,128,128]{2,1,0:T(8,128)}, f32[5,128,128]{2,1,0:T(8,128)S(1)}, u32[]{:S(2)}, u32[]{:S(2)}) collective-permute-start(f32[5,128,128]{2,1,0:T(8,128)} %get-tuple-element.38), channel_id=1, source_target_pairs={{1,2},{3,4},{5,6},{7,8},{9,10},{11,12},{13,14},{15,0},{2,1},{4,3},... | collective-permute-start | bytes 983048 | tf_op jit(solution)/shard_map/ppermute | solution.py:373
  10.7 8.0 %shard_map.140 = (f32[128,2,128]{2,1,0:T(2,128)}, f32[5,64,128]{2,1,0:T(8,128)}) custom-call(f32[5,256,128]{2,1,0:T(8,128)} %bitcast.10, f32[5,16,512]{2,1,0:T(8,128)} %back.1, s32[2,2048]{1,0:T(2,128)} %back_base.5, f32[2,8,2048]{2,1,0:T(8,128)} %back_weight.5, s32[2,4096]{1,0:T(2,128)} %blade_base.5, f32[2,8,4096]{2,1,0:T(8,128)} %blade_weight.5), custom_call_target="tpu_custom_call" | custom-call | flops 5000000000 | bytes 1556480 | tf_op jit(solution)/shard_map/pallas_call | solution.py:885
  18.8 6.5 %all-to-all-start = ((f32[128,2,128]{2,1,0:T(2,128)}), f32[128,2,128]{2,1,0:T(2,128)S(1)}, u32[]{:S(2)}, u32[]{:S(2)}) async-start(f32[128,2,128]{2,1,0:T(2,128)} %get-tuple-element.35), calls=%async_computation | async-start | bytes 262144 | tf_op jit(solution)/shard_map/all_to_all | solution.py:897
  25.3 1.1 collective-permute-start.2
  26.5 2.6 %collective-permute-start.3 = (f32[5,8,128]{2,1,0:T(8,128)S(1)}, f32[5,8,128]{2,1,0:T(8,128)S(1)}, u32[]{:S(2)}, u32[]{:S(2)}) collective-permute-start(f32[5,8,128]{2,1,0:T(8,128)S(1)} %copy-done.13), channel_id=1, source_target_pairs={{16,32},{48,64},{80,96},{32,16},{64,48},{96,80},{17,33},{49,65},{8... | collective-permute-start | bytes 61448 | tf_op jit(solution)/shard_map/ppermute | solution.py:372
  29.1 0.7 reshape.22.matrices
  29.8 0.0 collective-permute-done.2.got_x
  29.8 2.1 %collective-permute-done.3.got_x2 = f32[5,8,128]{2,1,0:T(8,128)S(1)} collective-permute-done((f32[5,8,128]{2,1,0:T(8,128)S(1)}, f32[5,8,128]{2,1,0:T(8,128)S(1)}, u32[]{:S(2)}, u32[]{:S(2)}) %collective-permute-start.3) | collective-permute-done | bytes 20512 | tf_op jit(solution)/shard_map/ppermute | solution.py:372
  31.9 0.0 collective-permute-done.got_y.old_y
  31.9 0.0 collective-permute-done.1.got_y2.old_y2
  31.9 0.6 copy-done.17
  32.5 0.1 copy-done.4
  32.6 0.1 copy-done.5
  32.7 8.0 %shard_map.142 = (f32[128,8,128]{2,1,0:T(8,128)}, f32[17,256,128]{2,1,0:T(8,128)}, f32[17,64,128]{2,1,0:T(8,128)}, s32[2,1,1024]{2,1,0:T(1,128)}, s32[2,1,2048]{2,1,0:T(1,128)}) custom-call(f32[6,25]{1,0:T(8,128)} %reshape.22.matrices, f32[5,256,128]{2,1,0:T(8,128)} %bitcast.7, f32[5,64,128]{2,1,0:T(8,128)} %get-tuple-element.36.cot_planes, ...), custom_call_target="tpu_custom_call" | custom-call | flops 2000000000 | bytes 4891224 | tf_op jit(solution)/shard_map/pallas_call | solution.py:885
  40.7 0.0 all-to-all-done.recv
  40.7 8.5 %all-to-all-start.1 = ((f32[128,8,128]{2,1,0:T(8,128)}), f32[128,8,128]{2,1,0:T(8,128)S(1)}, u32[]{:S(2)}, u32[]{:S(2)}) async-start(f32[128,8,128]{2,1,0:T(8,128)} %get-tuple-element.51), calls=%async_computation.1 | async-start | bytes 1048576 | tf_op jit(solution)/shard_map/all_to_all | solution.py:897
  49.3 3.6 %shard_map.143 = (f32[5,256,128]{2,1,0:T(8,128)}, f32[5,64,128]{2,1,0:T(8,128)}, f32[5,16,128]{2,1,0:T(8,128)}, f32[5,16,128]{2,1,0:T(8,128)}, f32[5,8,128]{2,1,0:T(8,128)}, /*index=5*/f32[5,8,128]{2,1,0:T(8,128)}) custom-call(f32[5,256,128]{2,1,0:T(8,128)} %bitcast.11, f32[5,64,128]{2,1,0:T(8,128)} %get-tuple-element.34.back_planes, ...), custom_call_target="tpu_custom_call" | custom-call | flops 1000000000 | bytes 1957888 | tf_op jit(solution)/shard_map/pallas_call | solution.py:885
  52.9 1.4 %collective-permute-start.4 = (f32[5,16,128]{2,1,0:T(8,128)}, f32[5,16,128]{2,1,0:T(8,128)S(1)}, u32[]{:S(2)}, u32[]{:S(2)}) collective-permute-start(f32[5,16,128]{2,1,0:T(8,128)} %get-tuple-element.45), channel_id=1, source_target_pairs={{0,1},{2,3},{4,5},{6,7},{8,9},{10,11},{12,13},{14,15},{1,0},{3,2},... | collective-permute-start | bytes 122888 | tf_op jit(solution)/shard_map/ppermute | solution.py:370
  54.3 4.7 %collective-permute-start.5 = (f32[5,16,128]{2,1,0:T(8,128)}, f32[5,16,128]{2,1,0:T(8,128)S(1)}, u32[]{:S(2)}, u32[]{:S(2)}) collective-permute-start(f32[5,16,128]{2,1,0:T(8,128)} %get-tuple-element.46), channel_id=1, source_target_pairs={{1,2},{3,4},{5,6},{7,8},{9,10},{11,12},{13,14},{15,0},{2,1},{4,3},... | collective-permute-start | bytes 122888 | tf_op jit(solution)/shard_map/ppermute | solution.py:373
  59.0 0.9 collective-permute-start.6
  59.9 3.0 %collective-permute-start.7 = (f32[5,8,128]{2,1,0:T(8,128)}, f32[5,8,128]{2,1,0:T(8,128)S(1)}, u32[]{:S(2)}, u32[]{:S(2)}) collective-permute-start(f32[5,8,128]{2,1,0:T(8,128)} %get-tuple-element.48), channel_id=1, source_target_pairs={{16,32},{48,64},{80,96},{32,16},{64,48},{96,80},{17,33},{49,65},{8... | collective-permute-start | bytes 61448 | tf_op jit(solution)/shard_map/ppermute | solution.py:372
  62.9 0.0 collective-permute-done.6.got_x
  62.9 2.3 %collective-permute-done.7.got_x2 = f32[5,8,128]{2,1,0:T(8,128)S(1)} collective-permute-done((f32[5,8,128]{2,1,0:T(8,128)}, f32[5,8,128]{2,1,0:T(8,128)S(1)}, u32[]{:S(2)}, u32[]{:S(2)}) %collective-permute-start.7) | collective-permute-done | bytes 20512 | tf_op jit(solution)/shard_map/ppermute | solution.py:372
  65.2 0.0 collective-permute-done.4.got_y
  65.2 0.0 collective-permute-done.5.got_y2
  65.2 0.0 all-to-all-done.1.recv
  65.3 0.5 copy-done.12
  65.8 0.0 copy-done.8
  65.8 0.0 copy-done.9
  65.9 0.2 copy-done
  66.0 20.6 %shard_map.144 = (f32[5,256,128]{2,1,0:T(8,128)}, f32[5,64,128]{2,1,0:T(8,128)}, f32[5,72,128]{2,1,0:T(8,128)}, f32[5,72,128]{2,1,0:T(8,128)}, f32[5,8,128]{2,1,0:T(8,128)}, /*index=5*/f32[5,8,128]{2,1,0:T(8,128)}) custom-call(f32[6,25]{1,0:T(8,128)} %reshape.22.matrices, f32[5,256,128]{2,1,0:T(8,128)} %get-tuple-element.43.blade_first, ...), custom_call_target="tpu_custom_call" | custom-call | flops 10000000000 | bytes 6595160 | tf_op jit(solution)/shard_map/pallas_call | solution.py:885
  86.7 0.1 collective-permute-start.8
  86.8 0.7 collective-permute-start.9
  87.5 1.8 %collective-permute-start.10 = (f32[5,8,128]{2,1,0:T(8,128)}, f32[5,8,128]{2,1,0:T(8,128)S(1)}, u32[]{:S(2)}, u32[]{:S(2)}) collective-permute-start(f32[5,8,128]{2,1,0:T(8,128)} %get-tuple-element.59), channel_id=1, source_target_pairs={{0,16},{32,48},{64,80},{96,112},{16,0},{48,32},{80,64},{112,96},{1... | collective-permute-start | bytes 61448 | tf_op jit(solution)/shard_map/ppermute | solution.py:371
  89.3 3.0 %collective-permute-start.11 = (f32[5,8,128]{2,1,0:T(8,128)}, f32[5,8,128]{2,1,0:T(8,128)S(1)}, u32[]{:S(2)}, u32[]{:S(2)}) collective-permute-start(f32[5,8,128]{2,1,0:T(8,128)} %get-tuple-element.60), channel_id=1, source_target_pairs={{16,32},{48,64},{80,96},{32,16},{64,48},{96,80},{17,33},{49,65},{8... | collective-permute-start | bytes 61448 | tf_op jit(solution)/shard_map/ppermute | solution.py:372
  92.3 4.2 %shard_map.145 = (f32[5,256,128]{2,1,0:T(8,128)}, f32[5,64,128]{2,1,0:T(8,128)}, f32[32,128]{1,0:T(8,128)}) custom-call(f32[6,25]{1,0:T(8,128)} %reshape.22.matrices, f32[5,256,128]{2,1,0:T(8,128)} %get-tuple-element.43.blade_first, f32[5,64,128]{2,1,0:T(8,128)} %get-tuple-element.44.back_first, f32[5,256,128]{2,1,0:T(8,128)} %get-tuple-element.52.blade_mid, ...), custom_call_target="tpu_custom_call" | custom-call | flops 1000000000 | bytes 2490968 | tf_op jit(solution)/shard_map/pallas_call | solution.py:885
  96.5 0.0 collective-permute-done.10.got_x
  96.5 0.0 collective-permute-done.8.got_y
  96.5 0.0 collective-permute-done.9.got_y2
  96.5 0.5 copy-done.11
  97.1 0.0 copy-done.14
  97.1 0.1 copy-done.6
  97.2 0.1 copy-done.7
  97.3 4.3 %shard_map.146 = (f32[128,2,128]{2,1,0:T(2,128)}, f32[5,256,128]{2,1,0:T(8,128)}, f32[5,64,128]{2,1,0:T(8,128)}) custom-call(f32[6,25]{1,0:T(8,128)} %reshape.22.matrices, f32[5,256,128]{2,1,0:T(8,128)} %get-tuple-element.43.blade_first, f32[5,64,128]{2,1,0:T(8,128)} %get-tuple-element.44.back_first, f32[5,256,128]{2,1,0:T(8,128)} %get-tuple-element.54.blade_part, ...), custom_call_target="tpu_custom_call" | custom-call | flops 1000000000 | bytes 3080792 | tf_op jit(solution)/shard_map/pallas_call | solution.py:885
  101.6 16.9 %all_to_all.15.recv = f32[128,2,128]{2,1,0:T(2,128)} all-to-all(f32[128,2,128]{2,1,0:T(2,128)} %get-tuple-element.63), channel_id=1, replica_groups=mesh['gx'=8,'gy'=16] {'gx','gy'}, dimensions={0} | all-to-all | bytes 262144 | tf_op jit(solution)/shard_map/all_to_all | solution.py:897
  118.5 8.9 %shard_map.147 = (f32[5,256,128]{2,1,0:T(8,128)}, f32[5,16,512]{2,1,0:T(8,128)}) custom-call(f32[5,256,128]{2,1,0:T(8,128)} %get-tuple-element.61.blade_kept, f32[5,64,128]{2,1,0:T(8,128)} %get-tuple-element.62.back_kept, f32[128,2,128]{2,1,0:T(2,128)} %all_to_all.15.recv, s32[2,2048]{1,0:T(2,128)} %back_base.5, f32[2,8,2048]{2,1,0:T(8,128)} %back_weight.5, ...), custom_call_target="tpu_custom_call" | custom-call | flops 5000000000 | bytes 2211840 | tf_op jit(solution)/shard_map/pallas_call | solution.py:885
  (28 shorter events, 0.1 us)
Async XLA Ops:
  3.2 28.7 %collective-permute-start = (f32[5,128,128]{2,1,0:T(8,128)}, f32[5,128,128]{2,1,0:T(8,128)S(1)}, u32[]{:S(2)}, u32[]{:S(2)}) collective-permute-start(f32[5,128,128]{2,1,0:T(8,128)} %get-tuple-element.37), channel_id=1, source_target_pairs={{0,1},{2,3},{4,5},{6,7},{8,9},{10,11},{12,13},{14,15},{1,0},{3,2},... | collective-permute-start | bytes 983048 | tf_op jit(solution)/shard_map/ppermute | solution.py:370
  5.3 20.0 %copy-start.15 = (f32[5,8,128]{2,1,0:T(8,128)S(1)}, f32[5,8,128]{2,1,0:T(8,128)}, u32[]{:S(2)}) copy-start(f32[5,8,128]{2,1,0:T(8,128)} %get-tuple-element.39) | copy-start | bytes 61444
  5.3 21.2 %copy-start.13 = (f32[5,8,128]{2,1,0:T(8,128)S(1)}, f32[5,8,128]{2,1,0:T(8,128)}, u32[]{:S(2)}) copy-start(f32[5,8,128]{2,1,0:T(8,128)} %get-tuple-element.40) | copy-start | bytes 61444
  5.3 23.8 %copy-start.2 = (f32[3,5,5]{2,0,1:T(4,128)S(1)}, f32[3,5,5]{2,0,1:T(4,128)}, u32[]{:S(2)}) copy-start(f32[3,5,5]{2,0,1:T(4,128)} %param.18) | copy-start | bytes 904
  5.3 23.8 %copy-start.3 = (f32[3,5,5]{2,0,1:T(4,128)S(1)}, f32[3,5,5]{2,0,1:T(4,128)}, u32[]{:S(2)}) copy-start(f32[3,5,5]{2,0,1:T(4,128)} %param.17) | copy-start | bytes 904
  5.3 26.6 %collective-permute-start.1 = (f32[5,128,128]{2,1,0:T(8,128)}, f32[5,128,128]{2,1,0:T(8,128)S(1)}, u32[]{:S(2)}, u32[]{:S(2)}) collective-permute-start(f32[5,128,128]{2,1,0:T(8,128)} %get-tuple-element.38), channel_id=1, source_target_pairs={{1,2},{3,4},{5,6},{7,8},{9,10},{11,12},{13,14},{15,0},{2,1},{4,3},... | collective-permute-start | bytes 983048 | tf_op jit(solution)/shard_map/ppermute | solution.py:373
  18.8 21.9 %all-to-all-start = ((f32[128,2,128]{2,1,0:T(2,128)}), f32[128,2,128]{2,1,0:T(2,128)S(1)}, u32[]{:S(2)}, u32[]{:S(2)}) async-start(f32[128,2,128]{2,1,0:T(2,128)} %get-tuple-element.35), calls=%async_computation | async-start | bytes 262144 | tf_op jit(solution)/shard_map/all_to_all | solution.py:897
  25.3 4.5 %collective-permute-start.2 = (f32[5,8,128]{2,1,0:T(8,128)S(1)}, f32[5,8,128]{2,1,0:T(8,128)S(1)}, u32[]{:S(2)}, u32[]{:S(2)}) collective-permute-start(f32[5,8,128]{2,1,0:T(8,128)S(1)} %copy-done.15), channel_id=1, source_target_pairs={{0,16},{32,48},{64,80},{96,112},{16,0},{48,32},{80,64},{112,96},{1... | collective-permute-start | bytes 61448 | tf_op jit(solution)/shard_map/ppermute | solution.py:371
  26.5 5.4 %collective-permute-start.3 = (f32[5,8,128]{2,1,0:T(8,128)S(1)}, f32[5,8,128]{2,1,0:T(8,128)S(1)}, u32[]{:S(2)}, u32[]{:S(2)}) collective-permute-start(f32[5,8,128]{2,1,0:T(8,128)S(1)} %copy-done.13), channel_id=1, source_target_pairs={{16,32},{48,64},{80,96},{32,16},{64,48},{96,80},{17,33},{49,65},{8... | collective-permute-start | bytes 61448 | tf_op jit(solution)/shard_map/ppermute | solution.py:372
  29.8 2.1 %copy-start.16 = (f32[5,8,128]{2,1,0:T(8,128)}, f32[5,8,128]{2,1,0:T(8,128)S(1)}, u32[]{:S(2)}) copy-start(f32[5,8,128]{2,1,0:T(8,128)S(1)} %collective-permute-done.2.got_x) | copy-start | bytes 61444
  31.9 0.6 copy-start.17
  31.9 0.7 copy-start.4
  31.9 0.8 copy-start.5
  40.7 8.6 %copy-start.1 = (f32[128,2,128]{2,1,0:T(2,128)}, f32[128,2,128]{2,1,0:T(2,128)S(1)}, u32[]{:S(2)}) copy-start(f32[128,2,128]{2,1,0:T(2,128)S(1)} %all-to-all-done.recv) | copy-start | bytes 393220
  40.7 24.5 %all-to-all-start.1 = ((f32[128,8,128]{2,1,0:T(8,128)}), f32[128,8,128]{2,1,0:T(8,128)S(1)}, u32[]{:S(2)}, u32[]{:S(2)}) async-start(f32[128,8,128]{2,1,0:T(8,128)} %get-tuple-element.51), calls=%async_computation.1 | async-start | bytes 1048576 | tf_op jit(solution)/shard_map/all_to_all | solution.py:897
  52.9 12.3 %collective-permute-start.4 = (f32[5,16,128]{2,1,0:T(8,128)}, f32[5,16,128]{2,1,0:T(8,128)S(1)}, u32[]{:S(2)}, u32[]{:S(2)}) collective-permute-start(f32[5,16,128]{2,1,0:T(8,128)} %get-tuple-element.45), channel_id=1, source_target_pairs={{0,1},{2,3},{4,5},{6,7},{8,9},{10,11},{12,13},{14,15},{1,0},{3,2},... | collective-permute-start | bytes 122888 | tf_op jit(solution)/shard_map/ppermute | solution.py:370
  54.3 10.9 %collective-permute-start.5 = (f32[5,16,128]{2,1,0:T(8,128)}, f32[5,16,128]{2,1,0:T(8,128)S(1)}, u32[]{:S(2)}, u32[]{:S(2)}) collective-permute-start(f32[5,16,128]{2,1,0:T(8,128)} %get-tuple-element.46), channel_id=1, source_target_pairs={{1,2},{3,4},{5,6},{7,8},{9,10},{11,12},{13,14},{15,0},{2,1},{4,3},... | collective-permute-start | bytes 122888 | tf_op jit(solution)/shard_map/ppermute | solution.py:373
  59.0 3.9 %collective-permute-start.6 = (f32[5,8,128]{2,1,0:T(8,128)}, f32[5,8,128]{2,1,0:T(8,128)S(1)}, u32[]{:S(2)}, u32[]{:S(2)}) collective-permute-start(f32[5,8,128]{2,1,0:T(8,128)} %get-tuple-element.47), channel_id=1, source_target_pairs={{0,16},{32,48},{64,80},{96,112},{16,0},{48,32},{80,64},{112,96},{1... | collective-permute-start | bytes 61448 | tf_op jit(solution)/shard_map/ppermute | solution.py:371
  59.9 5.3 %collective-permute-start.7 = (f32[5,8,128]{2,1,0:T(8,128)}, f32[5,8,128]{2,1,0:T(8,128)S(1)}, u32[]{:S(2)}, u32[]{:S(2)}) collective-permute-start(f32[5,8,128]{2,1,0:T(8,128)} %get-tuple-element.48), channel_id=1, source_target_pairs={{16,32},{48,64},{80,96},{32,16},{64,48},{96,80},{17,33},{49,65},{8... | collective-permute-start | bytes 61448 | tf_op jit(solution)/shard_map/ppermute | solution.py:372
  62.9 2.3 %copy-start.10 = (f32[5,8,128]{2,1,0:T(8,128)}, f32[5,8,128]{2,1,0:T(8,128)S(1)}, u32[]{:S(2)}) copy-start(f32[5,8,128]{2,1,0:T(8,128)S(1)} %collective-permute-done.6.got_x) | copy-start | bytes 61444
  65.2 0.6 copy-start.12
  65.2 0.6 copy-start.8
  65.2 0.6 copy-start.9
  65.2 0.8 copy-start
  86.7 9.8 %collective-permute-start.8 = (f32[5,72,128]{2,1,0:T(8,128)}, f32[5,72,128]{2,1,0:T(8,128)S(1)}, u32[]{:S(2)}, u32[]{:S(2)}) collective-permute-start(f32[5,72,128]{2,1,0:T(8,128)} %get-tuple-element.57), channel_id=1, source_target_pairs={{0,1},{2,3},{4,5},{6,7},{8,9},{10,11},{12,13},{14,15},{1,0},{3,2},... | collective-permute-start | bytes 552968 | tf_op jit(solution)/shard_map/ppermute | solution.py:370
  86.8 9.7 %collective-permute-start.9 = (f32[5,72,128]{2,1,0:T(8,128)}, f32[5,72,128]{2,1,0:T(8,128)S(1)}, u32[]{:S(2)}, u32[]{:S(2)}) collective-permute-start(f32[5,72,128]{2,1,0:T(8,128)} %get-tuple-element.58), channel_id=1, source_target_pairs={{1,2},{3,4},{5,6},{7,8},{9,10},{11,12},{13,14},{15,0},{2,1},{4,3},... | collective-permute-start | bytes 552968 | tf_op jit(solution)/shard_map/ppermute | solution.py:373
  87.5 9.0 %collective-permute-start.10 = (f32[5,8,128]{2,1,0:T(8,128)}, f32[5,8,128]{2,1,0:T(8,128)S(1)}, u32[]{:S(2)}, u32[]{:S(2)}) collective-permute-start(f32[5,8,128]{2,1,0:T(8,128)} %get-tuple-element.59), channel_id=1, source_target_pairs={{0,16},{32,48},{64,80},{96,112},{16,0},{48,32},{80,64},{112,96},{1... | collective-permute-start | bytes 61448 | tf_op jit(solution)/shard_map/ppermute | solution.py:371
  89.3 7.2 %collective-permute-start.11 = (f32[5,8,128]{2,1,0:T(8,128)}, f32[5,8,128]{2,1,0:T(8,128)S(1)}, u32[]{:S(2)}, u32[]{:S(2)}) collective-permute-start(f32[5,8,128]{2,1,0:T(8,128)} %get-tuple-element.60), channel_id=1, source_target_pairs={{16,32},{48,64},{80,96},{32,16},{64,48},{96,80},{17,33},{49,65},{8... | collective-permute-start | bytes 61448 | tf_op jit(solution)/shard_map/ppermute | solution.py:372
  96.5 0.6 copy-start.11
  96.5 0.6 copy-start.14
  96.5 0.7 copy-start.6
  96.5 0.8 copy-start.7
